TPU v7x, 256 devices: a whole 4x4x8 slice. The times are simulated.
256 devices in a mesh: row: 16 (over z, core), col: 16 (over x, y).
Axes of the slice: x: 4, y: 4, z: 8, core: 2. Of those that a mesh axis runs over, the one named last changes fastest.
Arguments:
- work: float32 [8192, 8192], P('row', 'col'), may hold values from -6 to 6
- a_tiles: bfloat16 [16, 16, 512, 512], P('row', None, 'col'), may hold values from -0.078125 to 0.078125
- b_tiles: bfloat16 [16, 16, 512, 512], P(None, 'col', 'row'), may hold values from -0.078125 to 0.078125
- u_powers: float32 [16, 3, 512, 512], P('row', None, 'col'), may hold values from -1 to 1, as said below
- v_powers: float32 [16, 3, 512, 512], P('col', None, 'row'), may hold values from -1 to 1, as said below
- shift: float32 [1], replicated, may hold values from 0.5 to 2
Outputs:
- progress: float32 [8192, 8192], P('row', 'col')
Inputs may be any that keep to these rules, and one draw needn't show every extreme that they name: u_powers[i] holds U, U^2 and U^4 for a lower triangular U whose diagonal entries have magnitudes 0.3 to 0.9. v_powers[j] holds V, V^2 and V^4 for an upper triangular V whose diagonal entries have magnitudes 0.3 to 0.9.
All inputs are finite; a program needn't handle non-finite values.
Results may differ from a plain program's by a relative error of at most 0.0023.
Values may be sent and summed in bfloat16 or wider, within the bound.
No kernel may reach another device: no remote copies, remote signals or barrier semaphores. Data moves between devices by JAX's collectives and lax.ppermute only.
A program may use at most 128 MiB of HBM per device.

v0:
```python
import jax
import jax.numpy as jnp
import numpy as np
from jax import lax
from jax.sharding import PartitionSpec as P

FRONTS = 3


finest = lax.Precision.HIGHEST


def in_order(blocks, dim):
    blocks = jnp.moveaxis(blocks, 0, dim)
    shape = blocks.shape
    return blocks.reshape(*shape[:dim], shape[dim] * shape[dim + 1], *shape[dim + 2 :])


def from_everyone(array, axis):
    copies = jnp.broadcast_to(array, (lax.axis_size(axis), *array.shape))
    return lax.all_to_all(copies, axis, split_axis=0, concat_axis=0, tiled=True)


def gathered_copies(array, axis, dim):
    return in_order(from_everyone(array, axis), dim)


def broadcast(array, axis, root):
    return lax.dynamic_index_in_dim(lax.all_gather(array, axis), root, 0, keepdims=False)


def product(left_side, right_side):
    return jnp.dot(left_side, right_side, preferred_element_type=jnp.float32, precision=finest)


def keep(source):
    return source


def per_device(work, a_tiles, b_tiles, u_powers, v_powers, shift):
    rows_count = lax.axis_size("row")
    cols_count = lax.axis_size("col")
    my_row = lax.axis_index("row")
    my_col = lax.axis_index("col")
    my_front = my_row + my_col
    first = max(0, (rows_count + cols_count) // 2 - FRONTS)
    width = work.shape[0]
    identity = jnp.eye(width, dtype=jnp.float32)
    shift_value = shift[0]
    u_base = gathered_copies(u_powers[:, :1], "col", 2)[0, 0]
    v_base = lax.all_gather(v_powers[:, :1], "row", axis=2, tiled=True)[0, 0]

    def powers_of():
        u_square = product(u_base, u_base)
        v_square = product(v_base, v_base)
        return (
            [u_base, u_square, product(u_square, u_square)],
            [v_base, v_square, product(v_square, v_square)],
        )

    def solve(source):
        u_list, v_list = powers_of()
        current = product(product(identity - u_list[0], source), identity - v_list[0]) / (
            2.0 * shift_value
        )
        for power in range(3):
            current = current + product(product(u_list[power], current), v_list[power])
        return current

    current = work
    for number in range(FRONTS):
        front = first + number
        current = lax.cond(my_front == front, solve, keep, current)
        sent = current.astype(jnp.bfloat16)
        down_row = front - my_col
        across_col = front - my_row
        valid_down = (down_row >= 0) & (down_row < rows_count)
        valid_across = (across_col >= 0) & (across_col < cols_count)
        down_clip = jnp.clip(down_row, 0, rows_count - 1)
        across_clip = jnp.clip(across_col, 0, cols_count - 1)
        down_tile = broadcast(sent, "row", down_clip)
        across_tile = broadcast(sent, "col", across_clip)
        a_rows = np.clip(front - np.arange(cols_count), 0, rows_count - 1).astype(np.int32)
        b_rows = np.clip(front - np.arange(rows_count), 0, cols_count - 1).astype(np.int32)
        a_tile = lax.all_to_all(
            a_tiles[0, a_rows], "col", split_axis=0, concat_axis=0, tiled=True
        ).reshape(width, width)
        b_tile = lax.all_to_all(
            b_tiles[b_rows, 0], "row", split_axis=0, concat_axis=0, tiled=True
        ).reshape(width, width)

        def update(source):
            minus_a = jnp.dot(a_tile, down_tile, preferred_element_type=jnp.float32)
            minus_b = jnp.dot(across_tile, b_tile, preferred_element_type=jnp.float32)
            return (
                source - jnp.where(valid_down, minus_a, 0.0) - jnp.where(valid_across, minus_b, 0.0)
            )

        current = lax.cond(my_front > front, update, keep, current)
    return current


def solution(mesh):
    placed = (
        P("row", "col"),
        P("row", None, "col", None),
        P(None, "col", "row", None),
        P("row", None, "col", None),
        P("col", None, "row", None),
        P(),
    )
    return jax.shard_map(
        per_device, mesh=mesh, in_specs=placed, out_specs=P("row", "col"), check_vma=False
    )
```

profile of v0, /device:TPU:70, one launch (start us, length us, event | category | flops | bytes accessed | tf_op | source)
XLA Modules:
  0.0 593.5 jit_solution(3004908231699741183)
XLA Ops:
  6.5 2.3 copy.78
  8.9 1.5 slice.10
  12.3 7.4 %all-to-all-start = ((f32[16,1,1,32,512]{4,3,2,1,0:T(8,128)}), f32[16,1,1,32,512]{4,3,2,1,0:T(8,128)S(1)}, u32[]{:S(2)}, u32[]{:S(2)}) async-start(f32[16,1,1,32,512]{4,3,2,1,0:T(8,128)} %broadcast_in_dim.35), calls=%async_computation | async-start | bytes 2097152 | tf_op jit(solution)/shard_map/all_to_all | solution.py:21
  20.9 14.1 %all-to-all-done = f32[16,1,1,32,512]{4,3,2,1,0:T(8,128)S(1)} async-done(((f32[16,1,1,32,512]{4,3,2,1,0:T(8,128)}), f32[16,1,1,32,512]{4,3,2,1,0:T(8,128)S(1)}, u32[]{:S(2)}, u32[]{:S(2)}) %all-to-all-start) | async-done | bytes 1048608 | tf_op jit(solution)/shard_map/all_to_all | solution.py:21
  35.0 14.5 %all-gather.14.cloned.1.call-done = f32[1,1,512,512]{3,2,1,0:T(8,128)} async-done(((f32[1,1,32,512]{3,2,1,0:T(8,128)}), f32[1,1,512,512]{3,2,1,0:T(8,128)}) %all-gather.14.cloned.1.call-update) | async-done | bytes 1048592 | tf_op jit(solution)/shard_map/all_gather | solution.py:51
  49.5 2.9 conditional.6
  52.4 2.2 convert_element_type.47
  55.3 1.4 gather_fusion
  56.7 33.7 %all-to-all-start.1 = ((bf16[16,32,512]{2,1,0:T(8,128)(2,1)}), bf16[16,32,512]{2,1,0:T(8,128)(2,1)}, u32[]{:S(2)}, u32[]{:S(2)}) async-start(bf16[16,32,512]{2,1,0:T(8,128)(2,1)} %gather_fusion), calls=%async_computation.1 | async-start | bytes 1048576 | tf_op jit(solution)/shard_map/all_to_all | solution.py:85
  90.4 1.4 gather_fusion.1
  91.8 8.6 %all-to-all-done.1 = bf16[16,32,512]{2,1,0:T(8,128)(2,1)} async-done(((bf16[16,32,512]{2,1,0:T(8,128)(2,1)}), bf16[16,32,512]{2,1,0:T(8,128)(2,1)}, u32[]{:S(2)}, u32[]{:S(2)}) %all-to-all-start.1) | async-done | bytes 524320 | tf_op jit(solution)/shard_map/all_to_all | solution.py:85
  100.4 10.2 %all-to-all-start.2 = ((bf16[16,32,512]{2,1,0:T(8,128)(2,1)}), bf16[16,32,512]{2,1,0:T(8,128)(2,1)}, u32[]{:S(2)}, u32[]{:S(2)}) async-start(bf16[16,32,512]{2,1,0:T(8,128)(2,1)} %gather_fusion.1), calls=%async_computation.2 | async-start | bytes 1048576 | tf_op jit(solution)/shard_map/all_to_all | solution.py:88
  110.6 14.9 %all-to-all-done.2 = bf16[16,32,512]{2,1,0:T(8,128)(2,1)} async-done(((bf16[16,32,512]{2,1,0:T(8,128)(2,1)}), bf16[16,32,512]{2,1,0:T(8,128)(2,1)}, u32[]{:S(2)}, u32[]{:S(2)}) %all-to-all-start.2) | async-done | bytes 524320 | tf_op jit(solution)/shard_map/all_to_all | solution.py:88
  125.5 31.5 %all-gather.18.cloned.1.call-done = bf16[8192,512]{1,0:T(8,128)(2,1)} async-done(((bf16[512,512]{1,0:T(8,128)(2,1)}), bf16[8192,512]{1,0:T(8,128)(2,1)}) %all-gather.18.cloned.1.call-update) | async-done | bytes 8388624 | tf_op jit(solution)/shard_map/all_gather | solution.py:29
  156.9 55.6 %all-gather.16.cloned.1.call-done = bf16[8192,512]{1,0:T(8,128)(2,1)} async-done(((bf16[512,512]{1,0:T(8,128)(2,1)}), bf16[8192,512]{1,0:T(8,128)(2,1)}) %all-gather.16.cloned.1.call-update) | async-done | bytes 8388624 | tf_op jit(solution)/shard_map/all_gather | solution.py:29
  212.6 8.5 %conditional.7 = (f32[512,512]{0,1:T(8,128)}) conditional(s32[]{:T(128)} %convert_element_type.44, (f32[512,512]{1,0:T(8,128)}) %conditional.6, (s32[]{:T(128)}, bf16[16,32,512]{2,1,0:T(8,128)(2,1)}, bf16[16,512,512]{2,1,0:T(8,128)(2,1)}, f32[512,512]{1,0:T(8,128)}, s32[]{:T(128)}, /*index=5*/bf16[16,512,512]{2,1,0:T(8,128)(2,1)}, ...), branch_computations={%region_2.3_spmd, %region_3.4_spmd.clone} | conditional | flops 537919488 | bytes 8388740 | solution.py:99
  212.6 2.7 convolution_select_fusion.2
  215.2 2.5 copy.45
  217.8 3.3 fusion.20
  221.1 5.2 conditional.8
  221.1 2.5 copy.61
  226.3 2.1 convert_element_type.48
  229.0 1.4 gather_fusion.2
  230.4 32.5 %all-to-all-start.3 = ((bf16[16,32,512]{2,1,0:T(8,128)(2,1)}), bf16[16,32,512]{2,1,0:T(8,128)(2,1)}, u32[]{:S(2)}, u32[]{:S(2)}) async-start(bf16[16,32,512]{2,1,0:T(8,128)(2,1)} %gather_fusion.2), calls=%async_computation.3 | async-start | bytes 1048576 | tf_op jit(solution)/shard_map/all_to_all | solution.py:85
  262.9 1.4 gather_fusion.3
  264.3 7.1 %all-to-all-done.3 = bf16[16,32,512]{2,1,0:T(8,128)(2,1)} async-done(((bf16[16,32,512]{2,1,0:T(8,128)(2,1)}), bf16[16,32,512]{2,1,0:T(8,128)(2,1)}, u32[]{:S(2)}, u32[]{:S(2)}) %all-to-all-start.3) | async-done | bytes 524320 | tf_op jit(solution)/shard_map/all_to_all | solution.py:85
  271.3 6.3 %all-to-all-start.4 = ((bf16[16,32,512]{2,1,0:T(8,128)(2,1)}), bf16[16,32,512]{2,1,0:T(8,128)(2,1)}, u32[]{:S(2)}, u32[]{:S(2)}) async-start(bf16[16,32,512]{2,1,0:T(8,128)(2,1)} %gather_fusion.3), calls=%async_computation.4 | async-start | bytes 1048576 | tf_op jit(solution)/shard_map/all_to_all | solution.py:88
  277.6 19.4 %all-to-all-done.4 = bf16[16,32,512]{2,1,0:T(8,128)(2,1)} async-done(((bf16[16,32,512]{2,1,0:T(8,128)(2,1)}), bf16[16,32,512]{2,1,0:T(8,128)(2,1)}, u32[]{:S(2)}, u32[]{:S(2)}) %all-to-all-start.4) | async-done | bytes 524320 | tf_op jit(solution)/shard_map/all_to_all | solution.py:88
  297.0 20.9 %all-gather.20.cloned.1.call-done = bf16[8192,512]{1,0:T(8,128)(2,1)} async-done(((bf16[512,512]{1,0:T(8,128)(2,1)}), bf16[8192,512]{1,0:T(8,128)(2,1)}) %all-gather.20.cloned.1.call-update) | async-done | bytes 8388624 | tf_op jit(solution)/shard_map/all_gather | solution.py:29
  317.9 78.5 %all-gather.22.cloned.1.call-done = bf16[8192,512]{1,0:T(8,128)(2,1)} async-done(((bf16[512,512]{1,0:T(8,128)(2,1)}), bf16[8192,512]{1,0:T(8,128)(2,1)}) %all-gather.22.cloned.1.call-update) | async-done | bytes 8388624 | tf_op jit(solution)/shard_map/all_gather | solution.py:29
  396.4 8.5 %conditional.9 = (f32[512,512]{0,1:T(8,128)}) conditional(s32[]{:T(128)} %convert_element_type.42, (f32[512,512]{1,0:T(8,128)}) %conditional.8, (s32[]{:T(128)}, bf16[16,32,512]{2,1,0:T(8,128)(2,1)}, bf16[16,512,512]{2,1,0:T(8,128)(2,1)}, f32[512,512]{1,0:T(8,128)}, s32[]{:T(128)}, /*index=5*/bf16[16,512,512]{2,1,0:T(8,128)(2,1)}, ...), branch_computations={%region_6.7_spmd, %region_7.8_spmd.clone} | conditional | flops 537919488 | bytes 8388740 | solution.py:99
  396.4 2.7 convolution_select_fusion.4
  399.1 2.5 copy.49
  401.6 3.3 fusion.29
  404.9 4.3 conditional.10
  404.9 1.6 copy.63
  410.9 1.4 gather_fusion.4
  412.3 30.6 %all-to-all-start.5 = ((bf16[16,32,512]{2,1,0:T(8,128)(2,1)}), bf16[16,32,512]{2,1,0:T(8,128)(2,1)S(1)}, u32[]{:S(2)}, u32[]{:S(2)}) async-start(bf16[16,32,512]{2,1,0:T(8,128)(2,1)} %gather_fusion.4), calls=%async_computation.5 | async-start | bytes 1048576 | tf_op jit(solution)/shard_map/all_to_all | solution.py:85
  442.8 1.4 gather_fusion.5
  444.2 8.2 %all-to-all-done.5 = bf16[16,32,512]{2,1,0:T(8,128)(2,1)S(1)} async-done(((bf16[16,32,512]{2,1,0:T(8,128)(2,1)}), bf16[16,32,512]{2,1,0:T(8,128)(2,1)S(1)}, u32[]{:S(2)}, u32[]{:S(2)}) %all-to-all-start.5) | async-done | bytes 524320 | tf_op jit(solution)/shard_map/all_to_all | solution.py:85
  452.4 6.2 %all-to-all-start.6 = ((bf16[16,32,512]{2,1,0:T(8,128)(2,1)}), bf16[16,32,512]{2,1,0:T(8,128)(2,1)S(1)}, u32[]{:S(2)}, u32[]{:S(2)}) async-start(bf16[16,32,512]{2,1,0:T(8,128)(2,1)} %gather_fusion.5), calls=%async_computation.6 | async-start | bytes 1048576 | tf_op jit(solution)/shard_map/all_to_all | solution.py:88
  458.6 19.4 %all-to-all-done.6 = bf16[16,32,512]{2,1,0:T(8,128)(2,1)S(1)} async-done(((bf16[16,32,512]{2,1,0:T(8,128)(2,1)}), bf16[16,32,512]{2,1,0:T(8,128)(2,1)S(1)}, u32[]{:S(2)}, u32[]{:S(2)}) %all-to-all-start.6) | async-done | bytes 524320 | tf_op jit(solution)/shard_map/all_to_all | solution.py:88
  477.9 21.0 %all-gather.24.cloned.1.call-done = bf16[8192,512]{1,0:T(8,128)(2,1)} async-done(((bf16[512,512]{1,0:T(8,128)(2,1)}), bf16[8192,512]{1,0:T(8,128)(2,1)}) %all-gather.24.cloned.1.call-update) | async-done | bytes 8388624 | tf_op jit(solution)/shard_map/all_gather | solution.py:29
  498.9 78.6 %all-gather.26.cloned.1.call-done = bf16[8192,512]{1,0:T(8,128)(2,1)} async-done(((bf16[512,512]{1,0:T(8,128)(2,1)}), bf16[8192,512]{1,0:T(8,128)(2,1)}) %all-gather.26.cloned.1.call-update) | async-done | bytes 8388624 | tf_op jit(solution)/shard_map/all_gather | solution.py:29
  577.6 6.1 %conditional.11 = (f32[512,512]{0,1:T(8,128)}) conditional(s32[]{:T(128)} %convert_element_type.40, (f32[512,512]{1,0:T(8,128)S(1)}) %conditional.10, (s32[]{:T(128)}, bf16[16,512,512]{2,1,0:T(8,128)(2,1)}, bf16[16,32,512]{2,1,0:T(8,128)(2,1)S(1)}, f32[512,512]{1,0:T(8,128)S(1)}, s32[]{:T(128)}, /*index=5*/bf16[16,512,512]{2,1,0:T(8,128)(2,1)}, ...), branch_computations={%region_10.11_spmd, %region_11.12_spmd} | conditional | flops 537919488 | bytes 10485920 | solution.py:99
  577.6 2.7 convolution_select_fusion
  580.6 3.0 fusion.11
  583.6 2.5 copy.54
  (33 shorter events, 6.5 us)
Async XLA Ops:
  6.5 48.8 %copy-start = (bf16[1,16,32,512]{3,2,1,0:T(8,128)(2,1)S(1)}, bf16[1,16,32,512]{3,2,1,0:T(8,128)(2,1)}, u32[]{:S(2)}) copy-start(bf16[1,16,32,512]{3,2,1,0:T(8,128)(2,1)} %param.31) | copy-start | bytes 1572868
  6.5 43.0 %all-gather.14.cloned.1.call-start = ((), (), s32[]{:S(2)}) async-start(), calls=%async_computation.7 | async-start | bytes 1114112 | tf_op jit(solution)/shard_map/all_gather | solution.py:51
  12.3 22.7 %all-to-all-start = ((f32[16,1,1,32,512]{4,3,2,1,0:T(8,128)}), f32[16,1,1,32,512]{4,3,2,1,0:T(8,128)S(1)}, u32[]{:S(2)}, u32[]{:S(2)}) async-start(f32[16,1,1,32,512]{4,3,2,1,0:T(8,128)} %broadcast_in_dim.35), calls=%async_computation | async-start | bytes 2097152 | tf_op jit(solution)/shard_map/all_to_all | solution.py:21
  19.8 137.2 %all-gather.18.cloned.1.call-start = ((), (), s32[]{:S(2)}) async-start(), calls=%async_computation.9 | async-start | bytes 8912896 | tf_op jit(solution)/shard_map/all_gather | solution.py:29
  49.5 5.8 copy-start.7
  49.5 40.9 %copy-start.3 = (bf16[16,1,32,512]{3,2,1,0:T(8,128)(2,1)S(1)}, bf16[16,1,32,512]{3,2,1,0:T(8,128)(2,1)}, u32[]{:S(2)}) copy-start(bf16[16,1,32,512]{3,2,1,0:T(8,128)(2,1)} %param.32) | copy-start | bytes 1572868
  52.4 168.7 %copy-start.1 = (f32[1,1,512,512]{3,2,1,0:T(8,128)S(1)}, f32[1,1,512,512]{3,2,1,0:T(8,128)}, u32[]{:S(2)}) copy-start(f32[1,1,512,512]{3,2,1,0:T(8,128)} %all-gather.14.cloned.1.call-done) | copy-start | bytes 3145732
  54.6 158.0 %all-gather.16.cloned.1.call-start = ((), (), s32[]{:S(2)}) async-start(), calls=%async_computation.8 | async-start | bytes 8912896 | tf_op jit(solution)/shard_map/all_gather | solution.py:29
  56.7 43.7 %all-to-all-start.1 = ((bf16[16,32,512]{2,1,0:T(8,128)(2,1)}), bf16[16,32,512]{2,1,0:T(8,128)(2,1)}, u32[]{:S(2)}, u32[]{:S(2)}) async-start(bf16[16,32,512]{2,1,0:T(8,128)(2,1)} %gather_fusion), calls=%async_computation.1 | async-start | bytes 1048576 | tf_op jit(solution)/shard_map/all_to_all | solution.py:85
  100.4 25.1 %all-to-all-start.2 = ((bf16[16,32,512]{2,1,0:T(8,128)(2,1)}), bf16[16,32,512]{2,1,0:T(8,128)(2,1)}, u32[]{:S(2)}, u32[]{:S(2)}) async-start(bf16[16,32,512]{2,1,0:T(8,128)(2,1)} %gather_fusion.1), calls=%async_computation.2 | async-start | bytes 1048576 | tf_op jit(solution)/shard_map/all_to_all | solution.py:88
  110.6 207.4 %all-gather.20.cloned.1.call-start = ((), (), s32[]{:S(2)}) async-start(), calls=%async_computation.10 | async-start | bytes 8912896 | tf_op jit(solution)/shard_map/all_gather | solution.py:29
  221.1 7.9 %copy-start.6 = (s32[16]{0:T(128)S(1)}, s32[16]{0:T(128)}, u32[]{:S(2)}) copy-start(s32[16]{0:T(128)} %constant.202) | copy-start | bytes 196
  228.4 168.0 %all-gather.22.cloned.1.call-start = ((), (), s32[]{:S(2)}) async-start(), calls=%async_computation.11 | async-start | bytes 8912896 | tf_op jit(solution)/shard_map/all_gather | solution.py:29
  230.4 40.9 %all-to-all-start.3 = ((bf16[16,32,512]{2,1,0:T(8,128)(2,1)}), bf16[16,32,512]{2,1,0:T(8,128)(2,1)}, u32[]{:S(2)}, u32[]{:S(2)}) async-start(bf16[16,32,512]{2,1,0:T(8,128)(2,1)} %gather_fusion.2), calls=%async_computation.3 | async-start | bytes 1048576 | tf_op jit(solution)/shard_map/all_to_all | solution.py:85
  271.3 25.7 %all-to-all-start.4 = ((bf16[16,32,512]{2,1,0:T(8,128)(2,1)}), bf16[16,32,512]{2,1,0:T(8,128)(2,1)}, u32[]{:S(2)}, u32[]{:S(2)}) async-start(bf16[16,32,512]{2,1,0:T(8,128)(2,1)} %gather_fusion.3), calls=%async_computation.4 | async-start | bytes 1048576 | tf_op jit(solution)/shard_map/all_to_all | solution.py:88
  277.6 221.3 %all-gather.24.cloned.1.call-start = ((), (), s32[]{:S(2)}) async-start(), calls=%async_computation.12 | async-start | bytes 8912896 | tf_op jit(solution)/shard_map/all_gather | solution.py:29
  404.9 5.9 %copy-start.5 = (s32[16]{0:T(128)S(1)}, s32[16]{0:T(128)}, u32[]{:S(2)}) copy-start(s32[16]{0:T(128)} %constant.218) | copy-start | bytes 196
  410.1 167.4 %all-gather.26.cloned.1.call-start = ((), (), s32[]{:S(2)}) async-start(), calls=%async_computation.13 | async-start | bytes 8912896 | tf_op jit(solution)/shard_map/all_gather | solution.py:29
  412.3 40.1 %all-to-all-start.5 = ((bf16[16,32,512]{2,1,0:T(8,128)(2,1)}), bf16[16,32,512]{2,1,0:T(8,128)(2,1)S(1)}, u32[]{:S(2)}, u32[]{:S(2)}) async-start(bf16[16,32,512]{2,1,0:T(8,128)(2,1)} %gather_fusion.4), calls=%async_computation.5 | async-start | bytes 1048576 | tf_op jit(solution)/shard_map/all_to_all | solution.py:85
  452.4 25.5 %all-to-all-start.6 = ((bf16[16,32,512]{2,1,0:T(8,128)(2,1)}), bf16[16,32,512]{2,1,0:T(8,128)(2,1)S(1)}, u32[]{:S(2)}, u32[]{:S(2)}) async-start(bf16[16,32,512]{2,1,0:T(8,128)(2,1)} %gather_fusion.5), calls=%async_computation.6 | async-start | bytes 1048576 | tf_op jit(solution)/shard_map/all_to_all | solution.py:88
  577.6 2.7 copy-start.4
Sparse Core Ops, SparseCore 0:
  10.5 38.9 all-gather.13
  54.7 102.1 all-gather.17
  158.8 53.7 all-gather.15
  228.5 89.3 all-gather.19
  320.2 76.1 all-gather.21
  410.2 88.6 all-gather.23
  501.3 76.1 all-gather.25
where the time goes:
time: 604 us; the launch traced here: 594 us
  waiting for transfers between devices  394 us (65%)
  starting transfers between devices  127 us (21%)
  local copies, waits for them, and re-layouts  26.1 us (4%)
  matrix products  17.7 us (3%)
  between operations  14.1 us (2%)
  loops' own time  8.24 us (1%)
  other arithmetic  6.23 us (1%)
    all_gather x6, waiting for transfers between devices, broadcast(): lax.all_gather(array, axis)  286 us
    all_to_all x3, starting transfers between devices, per_device(): lax.all_to_all(a_tiles[0, a_rows], 'col', split_axis=0, concat_axis=0, ti...  96.8 us
    all_to_all x3, waiting for transfers between devices, per_device(): lax.all_to_all(b_tiles[b_rows, 0], 'row', split_axis=0, concat_axis=0, ti...  53.6 us
    all_to_all x3, waiting for transfers between devices, per_device(): lax.all_to_all(a_tiles[0, a_rows], 'col', split_axis=0, concat_axis=0, ti...  23.9 us
    all_to_all x3, starting transfers between devices, per_device(): lax.all_to_all(b_tiles[b_rows, 0], 'row', split_axis=0, concat_axis=0, ti...  22.6 us
    all_gather x1, waiting for transfers between devices, per_device(): v_base = lax.all_gather(v_powers[:, :1], 'row', axis=2, tiled=True)[0, 0]  14.5 us
    all_to_all x1, waiting for transfers between devices, from_everyone(): return lax.all_to_all(copies, axis, split_axis=0, concat_axis=0, tiled=True)  14.1 us
  transfers between devices with their start and end apart: 14, of which 14 were waited for; matrix products, arithmetic and copies ran while one was open for 2% of the time, Pallas kernels for 0%

commit v1 on v0

v1 whole, which is shorter than its diff:
```python
import functools

import jax
import jax.numpy as jnp
import numpy as np
from jax import lax
from jax.experimental import pallas as pl
from jax.experimental.pallas import tpu as pltpu
from jax.sharding import PartitionSpec as P


FRONTS = 3
CORES = 2
INTERPRET = False
PLACE = pltpu.HBM

half_type = jnp.bfloat16
full_type = jnp.float32


class Grid:
    def __init__(self, rows, cols):
        self.rows, self.cols, self.deep = rows, cols, rows // CORES

    def place(self, i, j):
        return i * self.cols + j

    def front(self, number):
        return [(i, number - i) for i in range(self.rows) if 0 <= number - i < self.cols]

    def moved(self, number, down, right):
        return [
            (self.place(i, j), self.place(i + down, j + right))
            for i, j in self.front(number)
            if i + down < self.rows and j + right < self.cols
        ]

    def every(self, target_of, wanted):
        pairs = []
        for i in range(self.rows):
            for j in range(self.cols):
                k, l = target_of(i, j)
                if wanted(k, l):
                    pairs.append((self.place(i, j), self.place(k, l)))
        return pairs

    def deeper(self, step, wanted):
        return self.every(lambda i, j: ((i + CORES * step) % self.rows, j), wanted)

    def partner(self):
        return self.every(lambda i, j: (i ^ 1, j), lambda i, j: True)

    def tree(self, number, behind):
        steps = [[] for _ in range(self.deep.bit_length() - 1)]
        for i, j in self.front(number):
            root = i // CORES
            lowest = (behind - j + 1) // CORES
            for core in range(CORES):
                sign = 1 if core == 0 else -1

                def reach(at, level):
                    size = self.deep >> (level + 1)
                    if size == 0:
                        return at != root and at >= lowest
                    there = (at + sign * size) % self.deep
                    one = reach(at, level + 1)
                    return reach(there, level + 1) or one

                def walk(at, level):
                    size = self.deep >> (level + 1)
                    if size == 0:
                        return
                    there = (at + sign * size) % self.deep
                    if reach(there, level + 1):
                        steps[level].append(
                            (self.place(CORES * at + core, j), self.place(CORES * there + core, j))
                        )
                        walk(there, level + 1)
                    walk(at, level + 1)

                walk(root, 0)
        return steps


def exchange(array, axis):
    return lax.all_to_all(array, axis, split_axis=0, concat_axis=0, tiled=True)


def send(array, pairs):
    return lax.ppermute(array, ("row", "col"), pairs)


LOCAL = []


def settled(array):
    if any(array is one for one in LOCAL):
        return pltpu.with_memory_space_constraint(array, PLACE)
    return array


def kernel(body, outs, *operands, scalars=(), scratch=(), late=()):
    operands = [one if isinstance(one, tuple) else (one, None) for one in operands]
    parts = [
        (8, 128)
        if part == "raw"
        else one.shape if part is None else np.empty(one.shape, np.bool_)[part].shape
        for one, part in operands
    ]
    many, most = len(operands), 24

    def run(*refs):
        refs = list(refs)

        def take(count):
            taken, refs[:count] = refs[:count], []
            return taken

        given, inputs, results = take(len(scalars)), take(many), take(len(outs))
        held, made, (arrival, departure) = take(many), take(len(outs)), take(2)
        copies = []
        begun, waited, started = set(), set(), []
        for k, (one, part) in enumerate(operands):
            source = inputs[k] if part is None or part == "raw" else inputs[k].at[part]
            copies.append(
                None if part == "raw" else pltpu.make_async_copy(source, held[k], arrival.at[k])
            )

        def begin(k):
            if k not in begun:
                copies[k].start()
                begun.add(k)

        def load(k):
            if copies[k] is None:
                return inputs[k]
            begin(k)
            if k not in waited:
                copies[k].wait()
                waited.add(k)
            return held[k]

        load.begin = begin
        for k in range(many):
            if k not in late and copies[k] is not None:
                begin(k)

        def store(k, part=None):
            source, target = made[k], results[k]
            if part is not None:
                source, target = source.at[part], target.at[part]
            started.append(pltpu.make_async_copy(source, target, departure.at[len(started)]))
            started[-1].start()

        body(given, load, made, store, *refs)
        for k in range(many):
            load(k)
        for copy in started:
            copy.wait()

    made_here = pl.pallas_call(
        run,
        out_shape=[PLACE(shape, kind) for shape, kind in outs],
        in_specs=[pl.BlockSpec(memory_space=pltpu.SMEM)] * len(scalars)
        + [pl.BlockSpec(memory_space=pl.ANY)] * many,
        out_specs=[pl.BlockSpec(memory_space=PLACE)] * len(outs),
        scratch_shapes=[
            *(pltpu.VMEM(part, one.dtype) for part, (one, _) in zip(parts, operands)),
            *(pltpu.VMEM(shape, kind) for shape, kind in outs),
            pltpu.SemaphoreType.DMA((many,)),
            pltpu.SemaphoreType.DMA((most,)),
            *scratch,
        ],
        compiler_params=pltpu.CompilerParams(vmem_limit_bytes=48 * 1024 * 1024),
        interpret=INTERPRET,
    )(*scalars, *(settled(one) for one, _ in operands))
    LOCAL.extend(made_here)
    return made_here


def split(values):
    high = values.astype(half_type)
    return high, (values - high.astype(full_type)).astype(half_type)


def narrow(left_side, right_side):
    return jnp.dot(left_side, right_side, preferred_element_type=full_type)


def thrice(left_high, left_low, right_high, right_low):
    return (
        narrow(left_high, right_low)
        + narrow(left_low, right_high)
        + narrow(left_high, right_high)
    )


def lower_times(low_tri, values):
    middle = low_tri[0].shape[0] // 2
    high, low = split(values)
    top = thrice(
        low_tri[0][:middle, :middle], low_tri[1][:middle, :middle], high[:middle], low[:middle]
    )
    bottom = thrice(low_tri[0][middle:], low_tri[1][middle:], high, low)
    return jnp.concatenate([top, bottom], axis=0)


def times_upper(values, upp_tri):
    middle = upp_tri[0].shape[0] // 2
    high, low = split(values)
    left = thrice(
        high[:, :middle], low[:, :middle], upp_tri[0][:middle, :middle], upp_tri[1][:middle, :middle]
    )
    right = thrice(high, low, upp_tri[0][:, middle:], upp_tri[1][:, middle:])
    return jnp.concatenate([left, right], axis=1)


def solve(source, u_pair, v_pair, scale, u_more, v_more, solved_ref):
    right = source - lower_times(u_pair, source)
    solved_ref[...] = (right - times_upper(right, v_pair)) * scale
    moved = lower_times(u_pair, solved_ref[...])
    solved_ref[...] += times_upper(moved, v_pair)
    u_ref, v_ref = u_more(), v_more()

    def doubled(power, carry):
        moved = lower_times((u_ref[power, 0], u_ref[power, 1]), solved_ref[...])
        solved_ref[...] += times_upper(moved, (v_ref[power, 0], v_ref[power, 1]))
        return carry

    lax.fori_loop(0, 2, doubled, 0)


def opening_body(shape, scalars, load, made, store):
    first, rows, cols, deep, strip = shape
    (at,) = scalars
    out_ref, v_out, *b_outs = made
    u_ref = load(0)
    high, low = split(u_ref[0])
    a_ref = load(1)
    for c in range(cols):
        out_ref[c, :strip] = high
        out_ref[c, strip : 2 * strip] = low
        for n in range(FRONTS):
            out_ref[c, (2 + n) * strip : (3 + n) * strip] = a_ref[0, (first + n - c) % cols]
    store(0)
    high, low = split(load(2)[0])
    v_out[:strip] = high
    v_out[strip:] = low
    store(1)
    b_ref = load(3)
    for step in range(deep):
        there = (at[0] + step) % deep
        for k in range(FRONTS + 1):
            tile = (first + FRONTS - 1 - k - CORES * there + rows) % rows
            b_outs[step][k * strip : (k + 1) * strip] = b_ref[tile, 0]
        store(2 + step)


def sorted_v_body(deep, scalars, load, made, store):
    (at,) = scalars
    for step in range(deep):
        made[0][(at[0] - step + deep) % deep] = load(step)[...]
    store(0)


def sorted_b_body(deep, strip, scalars, load, made, store):
    (at,) = scalars
    keep_ref, give_ref = made
    core = at[1]
    for step in range(deep):
        source = (at[0] - step + deep) % deep
        ref = load(step)
        for n in range(FRONTS):
            k = FRONTS - 1 - n
            keep_ref[n, source] = ref[pl.ds((k + core) * strip, strip)]
            give_ref[n, source] = ref[pl.ds((k + 1 - core) * strip, strip)]
    store(1)
    store(0)


def joined(scr, core, keep_ref, got_ref):
    deep, _, width = keep_ref.shape
    for z in range(deep):
        scr[CORES * z + core] = keep_ref[z]
        scr[CORES * z + 1 - core] = got_ref[z]
    return scr[...].reshape(width, width)


def square_of(ref):
    return ref[...].reshape(ref.shape[-1], ref.shape[-1])


def first_body(shape, scalars, load, made, store, v_scr):
    deep, strip, width = shape
    at, scale = scalars
    u_ref, v_ref, solved_ref, sent_ref = made
    core = at[1]
    for z in range(deep):
        for part in range(2):
            rows = slice(part * strip, (part + 1) * strip)
            v_scr[part, CORES * z + core] = load(0)[z, rows]
            v_scr[part, CORES * z + 1 - core] = load(1)[z, rows]
    for part in range(2):
        v_ref[0, part] = v_scr[part].reshape(width, width)
        u_ref[0, part] = load(2)[:, part * strip : (part + 1) * strip].reshape(width, width)
    store(0, 0)
    store(1, 0)

    def squared(power, carry):
        base = (u_ref[power, 0], u_ref[power, 1])
        value = base[0].astype(full_type) + base[1].astype(full_type)
        u_ref[power + 1, 0], u_ref[power + 1, 1] = split(lower_times(base, value))
        base = (v_ref[power, 0], v_ref[power, 1])
        value = base[0].astype(full_type) + base[1].astype(full_type)
        v_ref[power + 1, 0], v_ref[power + 1, 1] = split(times_upper(value, base))
        return carry

    lax.fori_loop(0, 2, squared, 0)
    for power in (1, 2):
        store(0, power)
        store(1, power)
    solve(
        load(3)[...], (u_ref[0, 0], u_ref[0, 1]), (v_ref[0, 0], v_ref[0, 1]), scale[0],
        lambda: u_ref.at[1:], lambda: v_ref.at[1:], solved_ref,
    )
    sent_ref[...] = solved_ref[...].astype(half_type)
    store(3)
    store(2)


def next_body(count, scalars, load, made, store, b_scr):
    at, scale = scalars
    solved_ref, sent_ref, mine_ref, give_ref = made[:4]
    width = solved_ref.shape[0]
    half = width // 2
    core, root = at[1], at[6]
    base = 3 + 5 * count
    source = load(2)[...]
    for n in range(count):
        a_at, down_at, right_at, keep_at, got_at = range(3 + 5 * n, 8 + 5 * n)
        source = source - narrow(square_of(load(a_at)), load(down_at)[...])
        b_tile = joined(b_scr, core, load(keep_at), load(got_at))
        source = source - narrow(load(right_at)[...], b_tile)
    load.begin(base)
    load.begin(base + 1)
    u_ref, v_ref = load(0), load(1)
    solve(
        source, (u_ref[0], u_ref[1]), (v_ref[0], v_ref[1]), scale[0],
        lambda: load(base), lambda: load(base + 1), solved_ref,
    )
    sent_ref[...] = solved_ref[...].astype(half_type)
    store(1)
    tiles = [sent_ref] if mine_ref.shape[0] == 1 else [load(4), sent_ref]
    for n, tile in enumerate(tiles):

        @pl.when(root > 0)
        def _():
            mine_ref[n] = tile[pl.ds(core * half, half)]
            give_ref[n] = tile[pl.ds((1 - core) * half, half)]

        @pl.when(root == 0)
        def _():
            mine_ref[n] = jnp.zeros((half, width), half_type)
            give_ref[n] = jnp.zeros((half, width), half_type)

    if len(made) > 4:
        cols, twice, _ = made[4].shape
        strip = twice // 2
        made[4][:, :strip] = load(5)[...].reshape(cols, strip, width)
        made[4][:, strip:] = sent_ref[...].reshape(cols, strip, width)
        store(4)
    store(3)
    store(2)
    store(0)


def packed_body(scalars, load, made, store, piece, arrival):
    (at,) = scalars
    (out_ref,) = made
    cols, thrice_strip, _ = out_ref.shape
    strip = thrice_strip // 3
    come = pltpu.make_async_copy(load(0).at[at[2]], piece, arrival.at[0])
    come.start()
    out_ref[:, 2 * strip :] = load(1)[...].reshape(cols, strip, -1)
    come.wait()
    out_ref[:, : 2 * strip] = jnp.broadcast_to(piece[...], (cols, *piece.shape))
    store(0)


def fanned_body(scalars, load, made, store, piece, arrival):
    (at,) = scalars
    strip = piece.shape[0]
    come = pltpu.make_async_copy(load(0).at[at[2], pl.ds(2 * strip, strip)], piece, arrival.at[0])
    come.start()
    come.wait()
    made[0][...] = jnp.broadcast_to(piece[...], made[0].shape)
    store(0)


def taken_off(n, at, load, total, base, b_scr, d_scr):
    a_at, held_at, other_at, right_at, keep_at, got_at = range(base, base + 6)
    core = at[1]
    half, width = d_scr.shape[1:]
    d_scr[core] = load(held_at)[...].reshape(half, width)
    d_scr[1 - core] = load(other_at)[...].reshape(half, width)
    total[...] -= narrow(square_of(load(a_at)), d_scr[...].reshape(width, width))
    b_tile = joined(b_scr, core, load(keep_at), load(got_at))
    row_part = square_of(load(right_at))

    @pl.when(at[3 + n] > 0)
    def _():
        total[...] -= narrow(row_part, b_tile)


def behind_body(scalars, load, made, store, b_scr, d_scr):
    (at,) = scalars
    (total,) = made
    total[...] = load(0)[...]
    for n in range(FRONTS):

        @pl.when(at[7] == n)
        def _(ref=load(1 + n)):
            total[...] = ref[...]

    for k in range(4, 16):
        load(k)

    @pl.when(at[7] == FRONTS)
    def _():
        for n in range(2):
            taken_off(n, at, load, total, 4 + 6 * n, b_scr, d_scr)

    store(0)


def behind_last_body(scalars, load, made, store, b_scr, d_scr):
    (at,) = scalars
    (total,) = made
    total[...] = load(0)[...]
    for k in range(1, 7):
        load(k)

    @pl.when(at[7] == FRONTS)
    def _():
        taken_off(2, at, load, total, 1, b_scr, d_scr)

    store(0)


def sweep(work, a_tiles, b_tiles, u_powers, v_powers, shift):
    LOCAL[:] = [work, a_tiles, b_tiles, u_powers, v_powers]
    rows = lax.axis_size("row")
    cols = lax.axis_size("col")
    grid = Grid(rows, cols)
    deep = grid.deep
    i = lax.axis_index("row")
    j = lax.axis_index("col")
    z, core = i // CORES, i % CORES
    diagonal = i + j
    first = max(0, (rows + cols) // 2 - FRONTS)
    last = first + FRONTS - 1
    width = work.shape[0]
    strip = width // cols
    half = width // 2
    tile = (width, width)
    scale = 0.5 / shift

    def place(number):
        kind = jnp.clip(diagonal - first, -1, FRONTS)
        return jnp.stack(
            [z, core, jnp.clip(number - i, 0, cols - 1)]
            + [(i <= first + n).astype(jnp.int32) for n in range(FRONTS)]
            + [(diagonal == number).astype(jnp.int32), kind]
        ).astype(jnp.int32)

    at, at_second, at_last = place(first), place(first + 1), place(last)
    near = {n: set() for n in range(cols)}
    for n in range(FRONTS):
        for r, c in grid.front(first + n):
            near[c].add(r // CORES)
    opening, v_mine, *b_mine = kernel(
        functools.partial(opening_body, (first, rows, cols, deep, strip)),
        [((cols, (2 + FRONTS) * strip, width), half_type), ((2 * strip, width), half_type)]
        + [(((FRONTS + 1) * strip, width), half_type)] * deep,
        (u_powers, (0, slice(0, 1))),
        a_tiles,
        (v_powers, (0, slice(0, 1))),
        b_tiles,
        scalars=(at,),
    )
    opened = exchange(opening, "col")
    v_all = [v_mine] + [
        send(v_mine, grid.deeper(s, lambda k, l: k // CORES in near[l]))
        for s in range(1, deep)
    ]
    b_all = [b_mine[0]] + [
        send(b_mine[s], grid.deeper(s, lambda k, l: k // CORES * CORES + CORES - 1 + l > first))
        for s in range(1, deep)
    ]
    (v_here,) = kernel(
        functools.partial(sorted_v_body, deep), [((deep, 2 * strip, width), half_type)],
        *v_all, scalars=(at,),
    )
    v_there = send(v_here, grid.partner())

    powers = ((3, 2, *tile), half_type)
    u_list, v_list, x_first, s_first = kernel(
        functools.partial(first_body, (deep, strip, width)),
        [powers, powers, (tile, full_type), (tile, half_type)],
        v_here, v_there, (opened, (slice(None), slice(0, 2 * strip))), work,
        scalars=(at, scale), scratch=[pltpu.VMEM((2, rows, strip, width), half_type)],
    )
    hop_down = send(s_first, grid.moved(first, 1, 0))
    hop_right = send(s_first, grid.moved(first, 0, 1))
    far_down = send(s_first, grid.moved(first, 2, 0))
    far_right = send(s_first, grid.moved(first, 0, 2))
    b_keep, b_give = kernel(
        functools.partial(sorted_b_body, deep, strip),
        [((FRONTS, deep, strip, width), half_type)] * 2, *b_all, scalars=(at,),
    )
    b_got = send(b_give, grid.partner())

    def a_of(n):
        return opened, (slice(None), slice((2 + n) * strip, (3 + n) * strip))

    b_scr = pltpu.VMEM((rows, strip, width), half_type)
    d_scr = pltpu.VMEM((2, half, width), half_type)
    more = [(u_list, slice(1, 3)), (v_list, slice(1, 3))]

    halves = ((1, half, width), half_type)
    both = ((2, half, width), half_type)
    x_second, s_second, t_mine, t_give, third_operand = kernel(
        functools.partial(next_body, 1),
        [(tile, full_type), (tile, half_type), both, both, ((cols, 2 * strip, width), half_type)],
        (u_list, 0), (v_list, 0), work, a_of(0), hop_down, hop_right, (b_keep, 0), (b_got, 0), *more,
        scalars=(at_second, scale), scratch=[b_scr], late=(8, 9),
    )
    hop_down = send(s_second, grid.moved(first + 1, 1, 0))
    hop_right = send(s_second, grid.moved(first + 1, 0, 1))
    third = exchange(third_operand, "col")

    x_third, s_third, l_mine, l_give = kernel(
        functools.partial(next_body, 2),
        [(tile, full_type), (tile, half_type), halves, halves],
        (u_list, 0), (v_list, 0), work,
        a_of(0), far_down, far_right, (b_keep, 0), (b_got, 0),
        a_of(1), hop_down, hop_right, (b_keep, 1), (b_got, 1), *more,
        scalars=(at_last, scale), scratch=[b_scr], late=(13, 14),
    )
    one = pltpu.SemaphoreType.DMA((1,))
    (fourth_operand,) = kernel(
        packed_body, [((cols, 3 * strip, width), half_type)], (third, "raw"), s_third,
        scalars=(at_second,), scratch=[pltpu.VMEM((2 * strip, width), half_type), one],
    )
    fourth = exchange(fourth_operand, "col")
    (fifth_operand,) = kernel(
        fanned_body, [((cols, strip, width), half_type)], (fourth, "raw"),
        scalars=(at_last,), scratch=[pltpu.VMEM((strip, width), half_type), one],
    )
    fifth = exchange(fifth_operand, "col")

    def spread_deep(mine, give, number):
        given = send(give, grid.partner())
        held = mine + given
        for pairs in grid.tree(number, last):
            got = send(held, pairs)
            held = held + got
        return held, send(held, grid.partner())

    t_held, t_other = spread_deep(t_mine, t_give, first + 1)
    l_held, l_other = spread_deep(l_mine, l_give, last)

    factors = []
    for n in range(2):
        factors += [
            a_of(n), (t_held, n), (t_other, n),
            (fourth, (slice(None), slice(n * strip, (n + 1) * strip))), (b_keep, n), (b_got, n),
        ]
    (behind,) = kernel(
        behind_body, [(tile, full_type)], work, x_first, x_second, x_third, *factors,
        scalars=(at,), scratch=[b_scr, d_scr],
    )
    (result,) = kernel(
        behind_last_body, [(tile, full_type)],
        behind, a_of(2), l_held, l_other, fifth, (b_keep, 2), (b_got, 2),
        scalars=(at,), scratch=[b_scr, d_scr],
    )
    return result


def solution(mesh):
    placed = (
        P("row", "col"),
        P("row", None, "col", None),
        P(None, "col", "row", None),
        P("row", None, "col", None),
        P("col", None, "row", None),
        P(),
    )
    return jax.shard_map(
        sweep, mesh=mesh, in_specs=placed, out_specs=P("row", "col"), check_vma=False
    )
```

time: 604 us -> 221 us (0.37); the launches traced: 594 us -> 218 us
  waiting for transfers between devices: 394 us -> 32.8 us
  Pallas kernels: 0 us -> 62.5 us
  local copies, waits for them, and re-layouts: 26.1 us -> 4.71 us
  starting transfers between devices: 127 us -> 109 us
  matrix products: 17.7 us -> 0 us
  between operations: 14.1 us -> 1.46 us
  loops' own time: 8.24 us -> 0 us
    all_gather x7 -> x0, waiting for transfers between devices: 301 us -> none  [the longest x6 286 us: broadcast(): lax.all_gather(array, axis)]
    all_to_all x7 -> x4, waiting for transfers between devices: 91.5 us -> 0.01 us  [exchange(): return lax.all_to_all(array, axis, split_axis=0, concat_axis=0, tiled=True)]
    all_to_all x7 -> x4, starting transfers between devices: 127 us -> 58.7 us  [exchange(): return lax.all_to_all(array, axis, split_axis=0, concat_axis=0, tiled=True)]
    pallas_call x0 -> x10, Pallas kernels: none -> 62.5 us  [kernel(): pl.pallas_call(run, out_shape=[PLACE(shape, kind) for shape, kind in outs...]
    ppermute x0 -> x32, starting transfers between devices: none -> 50.8 us  [send(): return lax.ppermute(array, ('row', 'col'), pairs)]
    ppermute x0 -> x32, waiting for transfers between devices: none -> 32.8 us  [send(): return lax.ppermute(array, ('row', 'col'), pairs)]
    dot_general x6 -> x0, matrix products: 17.7 us -> none  [the longest x3 9.7 us: update(): minus_a = jnp.dot(a_tile, down_tile, preferred_element_type=jnp.float32)]
    gather x6 -> x0, local copies, waits for them, and re-layouts: 8.26 us -> none  [the longest x3 4.13 us: per_device(): a_tiles[0, a_rows]]
  transfers between devices with their start and end apart: 14 -> 36, of which waited for: 14 -> 5; matrix products, arithmetic and copies ran while one was open for 2% -> 3% of each run, Pallas kernels for 0% -> 19%
where the time goes in v1:
time: 221 us; the launch traced here: 218 us
  starting transfers between devices  109 us (49%)
  Pallas kernels  62.5 us (28%)
  waiting for transfers between devices  32.8 us (15%)
  other arithmetic  7.36 us (3%)
  local copies, waits for them, and re-layouts  4.71 us (2%)
    pallas_call x10, Pallas kernels, kernel(): pl.pallas_call(run, out_shape=[PLACE(shape, kind) for shape, kind in outs...  62.5 us
    all_to_all x4, starting transfers between devices, exchange(): return lax.all_to_all(array, axis, split_axis=0, concat_axis=0, tiled=True)  58.7 us
    ppermute x32, starting transfers between devices, send(): return lax.ppermute(array, ('row', 'col'), pairs)  50.8 us
    ppermute x32, waiting for transfers between devices, send(): return lax.ppermute(array, ('row', 'col'), pairs)  32.8 us
    unnamed x26, local copies, waits for them, and re-layouts  4.46 us
  transfers between devices with their start and end apart: 36, of which 5 were waited for; matrix products, arithmetic and copies ran while one was open for 3% of the time, Pallas kernels for 19%

profile of v1, /device:TPU:70, one launch (start us, length us, event | category | flops | bytes accessed | tf_op | source)
XLA Modules:
  0.0 218.3 jit_solution(3400160656928401066)
XLA Ops:
  0.1 3.9 %shard_map.64 = (bf16[16,160,512]{2,1,0:T(8,128)(2,1)}, bf16[64,512]{1,0:T(8,128)(2,1)}, bf16[128,512]{1,0:T(8,128)(2,1)}, bf16[128,512]{1,0:T(8,128)(2,1)}, bf1...) custom-call(s32[8]{0:T(128)S(1)} %stack.87.refs_0_, ...), custom_call_target="tpu_custom_call" | custom-call | tf_op jit(solution)/shard_map/pallas_call | solution.py:161
  4.1 7.6 %all-to-all-start = ((bf16[16,160,512]{2,1,0:T(8,128)(2,1)}), bf16[16,160,512]{2,1,0:T(8,128)(2,1)S(1)}, u32[]{:S(2)}, u32[]{:S(2)}) async-start(bf16[16,160,512]{2,1,0:T(8,128)(2,1)} %get-tuple-element.31), calls=%async_computation | async-start | bytes 5242880 | tf_op jit(solution)/shard_map/all_to_all | solution.py:86
  11.6 2.0 collective-permute-start.6
  13.7 1.3 collective-permute-start.5
  18.4 4.7 %collective-permute-start.10 = (bf16[128,512]{1,0:T(8,128)(2,1)}, bf16[128,512]{1,0:T(8,128)(2,1)S(1)}, u32[]{:S(2)}, u32[]{:S(2)}) collective-permute-start(bf16[128,512]{1,0:T(8,128)(2,1)} %get-tuple-element.37), channel_id=1, source_target_pairs={{11,43},{12,44},{13,45},{14,46},{15,47},{27,59},{28,60},{29,61},{3... | collective-permute-start | bytes 393224 | tf_op jit(solution)/shard_map/ppermute | solution.py:90
  23.1 6.7 %collective-permute-start.11 = (bf16[128,512]{1,0:T(8,128)(2,1)S(1)}, bf16[128,512]{1,0:T(8,128)(2,1)S(1)}, u32[]{:S(2)}, u32[]{:S(2)}) collective-permute-start(bf16[128,512]{1,0:T(8,128)(2,1)S(1)} %copy-done.12), channel_id=1, source_target_pairs={{9,73},{10,74},{11,75},{12,76},{13,77},{14,78},{15,79},{25,89},{26... | collective-permute-start | bytes 393224 | tf_op jit(solution)/shard_map/ppermute | solution.py:90
  29.9 2.5 %collective-permute-start.12 = (bf16[128,512]{1,0:T(8,128)(2,1)S(1)}, bf16[128,512]{1,0:T(8,128)(2,1)S(1)}, u32[]{:S(2)}, u32[]{:S(2)}) collective-permute-start(bf16[128,512]{1,0:T(8,128)(2,1)S(1)} %copy-done.11), channel_id=1, source_target_pairs={{7,103},{8,104},{9,105},{10,106},{11,107},{12,108},{13,109},{14,11... | collective-permute-start | bytes 393224 | tf_op jit(solution)/shard_map/ppermute | solution.py:90
  32.4 2.6 %shard_map.65.refs_2_ = bf16[8,64,512]{2,1,0:T(8,128)(2,1)} custom-call(s32[8]{0:T(128)S(1)} %stack.87.refs_0_, bf16[64,512]{1,0:T(8,128)(2,1)} %get-tuple-element.30.refs_1_, bf16[64,512]{1,0:T(8,128)(2,1)S(1)} %collective-permute-done.refs_2_, bf16[64,512]{1,0:T(8,128)(2,1)S(1)} %collective-permute-done.1.refs_3_, ...), custom_call_target="tpu_custom_call" | custom-call | tf_op jit(solution)/shard_map/pallas_call | solution.py:161
  35.1 5.7 %collective-permute-start.13 = (bf16[128,512]{1,0:T(8,128)(2,1)S(1)}, bf16[128,512]{1,0:T(8,128)(2,1)S(1)}, u32[]{:S(2)}, u32[]{:S(2)}) collective-permute-start(bf16[128,512]{1,0:T(8,128)(2,1)S(1)} %copy-done.10), channel_id=1, source_target_pairs={{5,133},{6,134},{7,135},{8,136},{9,137},{10,138},{11,139},{12,140}... | collective-permute-start | bytes 393224 | tf_op jit(solution)/shard_map/ppermute | solution.py:90
  40.8 3.2 %collective-permute-start.14 = (bf16[128,512]{1,0:T(8,128)(2,1)S(1)}, bf16[128,512]{1,0:T(8,128)(2,1)S(1)}, u32[]{:S(2)}, u32[]{:S(2)}) collective-permute-start(bf16[128,512]{1,0:T(8,128)(2,1)S(1)} %copy-done.9), channel_id=1, source_target_pairs={{3,163},{4,164},{5,165},{6,166},{7,167},{8,168},{9,169},{10,170},{... | collective-permute-start | bytes 393224 | tf_op jit(solution)/shard_map/ppermute | solution.py:90
  44.0 3.3 %collective-permute-done.11.refs_3_ = bf16[128,512]{1,0:T(8,128)(2,1)S(1)} collective-permute-done((bf16[128,512]{1,0:T(8,128)(2,1)S(1)}, bf16[128,512]{1,0:T(8,128)(2,1)S(1)}, u32[]{:S(2)}, u32[]{:S(2)}) %collective-permute-start.11) | collective-permute-done | bytes 131104 | tf_op jit(solution)/shard_map/ppermute | solution.py:90
  47.4 1.3 collective-permute-start.15
  48.7 1.9 collective-permute-start.16
  50.6 7.6 %collective-permute-done.14.refs_6_ = bf16[128,512]{1,0:T(8,128)(2,1)S(1)} collective-permute-done((bf16[128,512]{1,0:T(8,128)(2,1)S(1)}, bf16[128,512]{1,0:T(8,128)(2,1)S(1)}, u32[]{:S(2)}, u32[]{:S(2)}) %collective-permute-start.14) | collective-permute-done | bytes 131104 | tf_op jit(solution)/shard_map/ppermute | solution.py:90
  58.2 5.7 %collective-permute-done.15.refs_7_ = bf16[128,512]{1,0:T(8,128)(2,1)S(1)} collective-permute-done((bf16[128,512]{1,0:T(8,128)(2,1)S(1)}, bf16[128,512]{1,0:T(8,128)(2,1)S(1)}, u32[]{:S(2)}, u32[]{:S(2)}) %collective-permute-start.15) | collective-permute-done | bytes 131104 | tf_op jit(solution)/shard_map/ppermute | solution.py:90
  63.9 3.3 %shard_map.67 = (bf16[3,8,32,512]{3,2,1,0:T(8,128)(2,1)}, bf16[3,8,32,512]{3,2,1,0:T(8,128)(2,1)}) custom-call(s32[8]{0:T(128)S(1)} %stack.87.refs_0_, bf16[128,512]{1,0:T(8,128)(2,1)} %get-tuple-element.36.refs_1_, bf16[128,512]{1,0:T(8,128)(2,1)S(1)} %collective-permute-done.10.refs_2_, bf16[128,512]{1,0:T(8,128)(2,1)S(1)} %collective-permute-done.11.refs_3_, ...), custom_call_target="tpu_custom_call" | custom-call | tf_op jit(solution)/shard_map/pallas_call | solution.py:161
  68.8 1.0 copy-done.3
  69.9 12.0 %shard_map.66 = (bf16[3,2,512,512]{3,2,1,0:T(8,128)(2,1)}, bf16[3,2,512,512]{3,2,1,0:T(8,128)(2,1)}, f32[512,512]{1,0:T(8,128)}, bf16[512,512]{1,0:T(8,128)(2,1)}) custom-call(s32[8]{0:T(128)S(1)} %stack.87.refs_0_, f32[1]{0:T(128)S(6)} %div.14.refs_1_, bf16[8,64,512]{2,1,0:T(8,128)(2,1)} %shard_map.65.refs_2_, bf16[8,64,512]{2,1,0:T(8,128)(2,1)S(1)} %copy-done.3, ...), custom_call_target="tpu_custom_call" | custom-call | tf_op jit(solution)/shard_map/pallas_call | solution.py:161
  81.9 1.5 collective-permute-start.9
  83.4 1.5 collective-permute-start.8
  84.9 11.9 %shard_map.68 = (f32[512,512]{1,0:T(8,128)}, bf16[512,512]{1,0:T(8,128)(2,1)}, bf16[2,256,512]{2,1,0:T(8,128)(2,1)}, bf16[2,256,512]{2,1,0:T(8,128)(2,1)}, bf16[16,64,512]{2,1,0:T(8,128)(2,1)}) custom-call(s32[8]{0:T(128)S(1)} %stack.91.refs_0_, f32[1]{0:T(128)S(6)} %div.14.refs_1_, bf16[3,2,512,512]{3,2,1,0:T(8,128)(2,1)} %get-tuple-element.33.refs_2_.refs_10_.refs_15_, ...), custom_call_target="tpu_custom_call" | custom-call | tf_op jit(solution)/shard_map/pallas_call | solution.py:161
  96.8 15.9 %all-to-all-start.1 = ((bf16[16,64,512]{2,1,0:T(8,128)(2,1)}), bf16[16,64,512]{2,1,0:T(8,128)(2,1)}, u32[]{:S(2)}, u32[]{:S(2)}) async-start(bf16[16,64,512]{2,1,0:T(8,128)(2,1)} %get-tuple-element.51), calls=%async_computation.1 | async-start | bytes 2097152 | tf_op jit(solution)/shard_map/all_to_all | solution.py:86
  112.7 1.5 collective-permute-start.19
  114.2 1.5 collective-permute-start.18
  115.6 1.5 collective-permute-start.21
  117.1 1.4 collective-permute-start.20
  118.5 2.0 add.35
  120.5 1.5 collective-permute-start.23
  122.1 12.4 %shard_map.69 = (f32[512,512]{1,0:T(8,128)}, bf16[512,512]{1,0:T(8,128)(2,1)}, bf16[1,256,512]{2,1,0:T(8,128)(2,1)}, bf16[1,256,512]{2,1,0:T(8,128)(2,1)}) custom-call(s32[8]{0:T(128)S(1)} %stack.95.refs_0_, f32[1]{0:T(128)S(6)} %div.14.refs_1_, bf16[3,2,512,512]{3,2,1,0:T(8,128)(2,1)} %get-tuple-element.33.refs_2_.refs_10_.refs_15_, ...), custom_call_target="tpu_custom_call" | custom-call | tf_op jit(solution)/shard_map/pallas_call | solution.py:161
  134.6 3.1 %shard_map.70 = bf16[16,96,512]{2,1,0:T(8,128)(2,1)} custom-call(s32[8]{0:T(128)S(1)} %stack.91.refs_0_, bf16[16,64,512]{2,1,0:T(8,128)(2,1)} %all-to-all-done.1.refs_1_, bf16[512,512]{1,0:T(8,128)(2,1)} %get-tuple-element.52.refs_2_), custom_call_target="tpu_custom_call" | custom-call | tf_op jit(solution)/shard_map/pallas_call | solution.py:161
  137.7 19.5 %all-to-all-start.2 = ((bf16[16,96,512]{2,1,0:T(8,128)(2,1)}), bf16[16,96,512]{2,1,0:T(8,128)(2,1)}, u32[]{:S(2)}, u32[]{:S(2)}) async-start(bf16[16,96,512]{2,1,0:T(8,128)(2,1)} %shard_map.70), calls=%async_computation.2 | async-start | bytes 3145728 | tf_op jit(solution)/shard_map/all_to_all | solution.py:86
  157.1 1.3 add.36
  159.2 1.1 collective-permute-start.27
  160.2 1.4 collective-permute-done.27
  161.6 1.0 add.39
  162.8 1.3 collective-permute-start.25
  165.5 14.7 %collective-permute-done.25 = bf16[2,256,512]{2,1,0:T(8,128)(2,1)S(1)} collective-permute-done((bf16[2,256,512]{2,1,0:T(8,128)(2,1)S(1)}, bf16[2,256,512]{2,1,0:T(8,128)(2,1)S(1)}, u32[]{:S(2)}, u32[]{:S(2)}) %collective-permute-start.25) | collective-permute-done | bytes 524320 | tf_op jit(solution)/shard_map/ppermute | solution.py:90
  180.2 0.9 add.38.refs_6_.refs_12_
  181.3 0.8 add.41
  182.1 1.3 collective-permute-start.30
  183.4 2.4 %shard_map.72 = bf16[16,32,512]{2,1,0:T(8,128)(2,1)} custom-call(s32[8]{0:T(128)S(1)} %stack.95.refs_0_, bf16[16,96,512]{2,1,0:T(8,128)(2,1)} %all-to-all-done.2.refs_8_.refs_14_.refs_1_), custom_call_target="tpu_custom_call" | custom-call | tf_op jit(solution)/shard_map/pallas_call | solution.py:161
  185.8 15.8 %all-to-all-start.3 = ((bf16[16,32,512]{2,1,0:T(8,128)(2,1)}), bf16[16,32,512]{2,1,0:T(8,128)(2,1)}, u32[]{:S(2)}, u32[]{:S(2)}) async-start(bf16[16,32,512]{2,1,0:T(8,128)(2,1)} %shard_map.72), calls=%async_computation.3 | async-start | bytes 1048576 | tf_op jit(solution)/shard_map/all_to_all | solution.py:86
  201.6 1.1 add.42.refs_3_
  202.7 1.9 collective-permute-start.31
  204.6 6.7 %shard_map.71.refs_1_ = f32[512,512]{1,0:T(8,128)} custom-call(s32[8]{0:T(128)S(1)} %stack.87.refs_0_, f32[512,512]{1,0:T(8,128)} %refs_1_.3, f32[512,512]{1,0:T(8,128)} %get-tuple-element.32.refs_2_, f32[512,512]{1,0:T(8,128)} %get-tuple-element.46.refs_3_, f32[512,512]{1,0:T(8,128)} %get-tuple-element.48.refs_4_, ...), custom_call_target="tpu_custom_call" | custom-call | tf_op jit(solution)/shard_map/pallas_call | solution.py:161
  212.0 0.9 copy-done.1
  213.0 0.9 copy-done.5
  213.9 4.2 %shard_map.73 = f32[512,512]{1,0:T(8,128)} custom-call(s32[8]{0:T(128)S(1)} %stack.87.refs_0_, f32[512,512]{1,0:T(8,128)} %shard_map.71.refs_1_, bf16[16,160,512]{2,1,0:T(8,128)(2,1)S(1)} %all-to-all-done.refs_4_.refs_5_.refs_10_.refs_11_.refs_2_, bf16[1,256,512]{2,1,0:T(8,128)(2,1)S(1)} %copy-done.1, bf16[1,256,512]{2,1,0:T(8,128)(2,1)S(1)} %copy-done.5, ...), custom_call_target="tpu_custom_call" | custom-call | tf_op jit(solution)/shard_map/pallas_call | solution.py:161
  (71 shorter events, 7.7 us)
Async XLA Ops:
  4.0 7.6 %copy-start.6 = (bf16[64,512]{1,0:T(8,128)(2,1)S(1)}, bf16[64,512]{1,0:T(8,128)(2,1)}, u32[]{:S(2)}) copy-start(bf16[64,512]{1,0:T(8,128)(2,1)} %get-tuple-element.30.refs_1_) | copy-start | bytes 196612
  4.0 19.1 %copy-start.12 = (bf16[128,512]{1,0:T(8,128)(2,1)S(1)}, bf16[128,512]{1,0:T(8,128)(2,1)}, u32[]{:S(2)}) copy-start(bf16[128,512]{1,0:T(8,128)(2,1)} %get-tuple-element.38) | copy-start | bytes 393220
  4.0 25.9 %copy-start.11 = (bf16[128,512]{1,0:T(8,128)(2,1)S(1)}, bf16[128,512]{1,0:T(8,128)(2,1)}, u32[]{:S(2)}) copy-start(bf16[128,512]{1,0:T(8,128)(2,1)} %get-tuple-element.39) | copy-start | bytes 393220
  4.0 31.1 %copy-start.10 = (bf16[128,512]{1,0:T(8,128)(2,1)S(1)}, bf16[128,512]{1,0:T(8,128)(2,1)}, u32[]{:S(2)}) copy-start(bf16[128,512]{1,0:T(8,128)(2,1)} %get-tuple-element.40) | copy-start | bytes 393220
  4.0 36.8 %copy-start.9 = (bf16[128,512]{1,0:T(8,128)(2,1)S(1)}, bf16[128,512]{1,0:T(8,128)(2,1)}, u32[]{:S(2)}) copy-start(bf16[128,512]{1,0:T(8,128)(2,1)} %get-tuple-element.41) | copy-start | bytes 393220
  4.0 43.3 %copy-start.8 = (bf16[128,512]{1,0:T(8,128)(2,1)S(1)}, bf16[128,512]{1,0:T(8,128)(2,1)}, u32[]{:S(2)}) copy-start(bf16[128,512]{1,0:T(8,128)(2,1)} %get-tuple-element.42) | copy-start | bytes 393220
  4.0 44.6 %copy-start.7 = (bf16[128,512]{1,0:T(8,128)(2,1)S(1)}, bf16[128,512]{1,0:T(8,128)(2,1)}, u32[]{:S(2)}) copy-start(bf16[128,512]{1,0:T(8,128)(2,1)} %get-tuple-element.43) | copy-start | bytes 393220
  4.1 64.8 %all-to-all-start = ((bf16[16,160,512]{2,1,0:T(8,128)(2,1)}), bf16[16,160,512]{2,1,0:T(8,128)(2,1)S(1)}, u32[]{:S(2)}, u32[]{:S(2)}) async-start(bf16[16,160,512]{2,1,0:T(8,128)(2,1)} %get-tuple-element.31), calls=%async_computation | async-start | bytes 5242880 | tf_op jit(solution)/shard_map/all_to_all | solution.py:86
  11.6 5.3 %collective-permute-start.6 = (bf16[64,512]{1,0:T(8,128)(2,1)S(1)}, bf16[64,512]{1,0:T(8,128)(2,1)S(1)}, u32[]{:S(2)}, u32[]{:S(2)}) collective-permute-start(bf16[64,512]{1,0:T(8,128)(2,1)S(1)} %copy-done.6), channel_id=1, source_target_pairs={{0,224},{1,225},{16,240},{17,241},{44,12},{45,13},{46,14},{47,15},... | collective-permute-start | bytes 196616 | tf_op jit(solution)/shard_map/ppermute | solution.py:90
  13.7 4.0 %collective-permute-start.5 = (bf16[64,512]{1,0:T(8,128)(2,1)S(1)}, bf16[64,512]{1,0:T(8,128)(2,1)S(1)}, u32[]{:S(2)}, u32[]{:S(2)}) collective-permute-start(bf16[64,512]{1,0:T(8,128)(2,1)S(1)} %copy-done.6), channel_id=1, source_target_pairs={{0,192},{1,193},{2,194},{3,195},{16,208},{17,209},{18,210},{19,211... | collective-permute-start | bytes 196616 | tf_op jit(solution)/shard_map/ppermute | solution.py:90
  15.0 3.4 %collective-permute-start.4 = (bf16[64,512]{1,0:T(8,128)(2,1)S(1)}, bf16[64,512]{1,0:T(8,128)(2,1)S(1)}, u32[]{:S(2)}, u32[]{:S(2)}) collective-permute-start(bf16[64,512]{1,0:T(8,128)(2,1)S(1)} %copy-done.6), channel_id=1, source_target_pairs={{2,162},{3,163},{4,164},{5,165},{18,178},{19,179},{20,180},{21,181... | collective-permute-start | bytes 196616 | tf_op jit(solution)/shard_map/ppermute | solution.py:90
  15.6 7.5 %collective-permute-start.3 = (bf16[64,512]{1,0:T(8,128)(2,1)S(1)}, bf16[64,512]{1,0:T(8,128)(2,1)S(1)}, u32[]{:S(2)}, u32[]{:S(2)}) collective-permute-start(bf16[64,512]{1,0:T(8,128)(2,1)S(1)} %copy-done.6), channel_id=1, source_target_pairs={{4,132},{5,133},{6,134},{7,135},{20,148},{21,149},{22,150},{23,151... | collective-permute-start | bytes 196616 | tf_op jit(solution)/shard_map/ppermute | solution.py:90
  16.3 13.5 %collective-permute-start.2 = (bf16[64,512]{1,0:T(8,128)(2,1)S(1)}, bf16[64,512]{1,0:T(8,128)(2,1)S(1)}, u32[]{:S(2)}, u32[]{:S(2)}) collective-permute-start(bf16[64,512]{1,0:T(8,128)(2,1)S(1)} %copy-done.6), channel_id=1, source_target_pairs={{6,102},{7,103},{8,104},{9,105},{22,118},{23,119},{24,120},{25,121... | collective-permute-start | bytes 196616 | tf_op jit(solution)/shard_map/ppermute | solution.py:90
  17.0 15.4 %collective-permute-start.1 = (bf16[64,512]{1,0:T(8,128)(2,1)S(1)}, bf16[64,512]{1,0:T(8,128)(2,1)S(1)}, u32[]{:S(2)}, u32[]{:S(2)}) collective-permute-start(bf16[64,512]{1,0:T(8,128)(2,1)S(1)} %copy-done.6), channel_id=1, source_target_pairs={{8,72},{9,73},{10,74},{11,75},{24,88},{25,89},{26,90},{27,91},{38,... | collective-permute-start | bytes 196616 | tf_op jit(solution)/shard_map/ppermute | solution.py:90
  17.7 14.8 %collective-permute-start = (bf16[64,512]{1,0:T(8,128)(2,1)S(1)}, bf16[64,512]{1,0:T(8,128)(2,1)S(1)}, u32[]{:S(2)}, u32[]{:S(2)}) collective-permute-start(bf16[64,512]{1,0:T(8,128)(2,1)S(1)} %copy-done.6), channel_id=1, source_target_pairs={{10,42},{11,43},{12,44},{13,45},{26,58},{27,59},{28,60},{29,61},{4... | collective-permute-start | bytes 196616 | tf_op jit(solution)/shard_map/ppermute | solution.py:90
  18.4 22.5 %collective-permute-start.10 = (bf16[128,512]{1,0:T(8,128)(2,1)}, bf16[128,512]{1,0:T(8,128)(2,1)S(1)}, u32[]{:S(2)}, u32[]{:S(2)}) collective-permute-start(bf16[128,512]{1,0:T(8,128)(2,1)} %get-tuple-element.37), channel_id=1, source_target_pairs={{11,43},{12,44},{13,45},{14,46},{15,47},{27,59},{28,60},{29,61},{3... | collective-permute-start | bytes 393224 | tf_op jit(solution)/shard_map/ppermute | solution.py:90
  23.1 24.2 %collective-permute-start.11 = (bf16[128,512]{1,0:T(8,128)(2,1)S(1)}, bf16[128,512]{1,0:T(8,128)(2,1)S(1)}, u32[]{:S(2)}, u32[]{:S(2)}) collective-permute-start(bf16[128,512]{1,0:T(8,128)(2,1)S(1)} %copy-done.12), channel_id=1, source_target_pairs={{9,73},{10,74},{11,75},{12,76},{13,77},{14,78},{15,79},{25,89},{26... | collective-permute-start | bytes 393224 | tf_op jit(solution)/shard_map/ppermute | solution.py:90
  29.9 18.8 %collective-permute-start.12 = (bf16[128,512]{1,0:T(8,128)(2,1)S(1)}, bf16[128,512]{1,0:T(8,128)(2,1)S(1)}, u32[]{:S(2)}, u32[]{:S(2)}) collective-permute-start(bf16[128,512]{1,0:T(8,128)(2,1)S(1)} %copy-done.11), channel_id=1, source_target_pairs={{7,103},{8,104},{9,105},{10,106},{11,107},{12,108},{13,109},{14,11... | collective-permute-start | bytes 393224 | tf_op jit(solution)/shard_map/ppermute | solution.py:90
  35.0 33.0 %collective-permute-start.7 = (bf16[8,64,512]{2,1,0:T(8,128)(2,1)}, bf16[8,64,512]{2,1,0:T(8,128)(2,1)S(1)}, u32[]{:S(2)}, u32[]{:S(2)}) collective-permute-start(bf16[8,64,512]{2,1,0:T(8,128)(2,1)} %shard_map.65.refs_2_), channel_id=1, source_target_pairs={{0,16},{1,17},{2,18},{3,19},{4,20},{5,21},{6,22},{7,23},{8,24},{9,... | collective-permute-start | bytes 1572872 | tf_op jit(solution)/shard_map/ppermute | solution.py:90
  35.1 15.5 %collective-permute-start.13 = (bf16[128,512]{1,0:T(8,128)(2,1)S(1)}, bf16[128,512]{1,0:T(8,128)(2,1)S(1)}, u32[]{:S(2)}, u32[]{:S(2)}) collective-permute-start(bf16[128,512]{1,0:T(8,128)(2,1)S(1)} %copy-done.10), channel_id=1, source_target_pairs={{5,133},{6,134},{7,135},{8,136},{9,137},{10,138},{11,139},{12,140}... | collective-permute-start | bytes 393224 | tf_op jit(solution)/shard_map/ppermute | solution.py:90
  40.8 17.4 %collective-permute-start.14 = (bf16[128,512]{1,0:T(8,128)(2,1)S(1)}, bf16[128,512]{1,0:T(8,128)(2,1)S(1)}, u32[]{:S(2)}, u32[]{:S(2)}) collective-permute-start(bf16[128,512]{1,0:T(8,128)(2,1)S(1)} %copy-done.9), channel_id=1, source_target_pairs={{3,163},{4,164},{5,165},{6,166},{7,167},{8,168},{9,169},{10,170},{... | collective-permute-start | bytes 393224 | tf_op jit(solution)/shard_map/ppermute | solution.py:90
  47.4 16.6 %collective-permute-start.15 = (bf16[128,512]{1,0:T(8,128)(2,1)S(1)}, bf16[128,512]{1,0:T(8,128)(2,1)S(1)}, u32[]{:S(2)}, u32[]{:S(2)}) collective-permute-start(bf16[128,512]{1,0:T(8,128)(2,1)S(1)} %copy-done.8), channel_id=1, source_target_pairs={{1,193},{2,194},{3,195},{4,196},{5,197},{6,198},{7,199},{8,200},{9... | collective-permute-start | bytes 393224 | tf_op jit(solution)/shard_map/ppermute | solution.py:90
  48.7 15.3 %collective-permute-start.16 = (bf16[128,512]{1,0:T(8,128)(2,1)S(1)}, bf16[128,512]{1,0:T(8,128)(2,1)S(1)}, u32[]{:S(2)}, u32[]{:S(2)}) collective-permute-start(bf16[128,512]{1,0:T(8,128)(2,1)S(1)} %copy-done.7), channel_id=1, source_target_pairs={{0,224},{1,225},{2,226},{3,227},{4,228},{5,229},{6,230},{7,231},{8... | collective-permute-start | bytes 393224 | tf_op jit(solution)/shard_map/ppermute | solution.py:90
  67.2 17.7 %collective-permute-start.17 = (bf16[3,8,32,512]{3,2,1,0:T(8,128)(2,1)}, bf16[3,8,32,512]{3,2,1,0:T(8,128)(2,1)S(1)}, u32[]{:S(2)}, u32[]{:S(2)}) collective-permute-start(bf16[3,8,32,512]{3,2,1,0:T(8,128)(2,1)} %get-tuple-element.45), channel_id=1, source_target_pairs={{0,16},{1,17},{2,18},{3,19},{4,20},{5,21},{6,22},{7,23},{8,24},{9,... | collective-permute-start | bytes 2359304 | tf_op jit(solution)/shard_map/ppermute | solution.py:90
  68.0 0.8 copy-start.2
  68.8 1.0 copy-start.3
  81.9 3.0 %collective-permute-start.9 = (bf16[512,512]{1,0:T(8,128)(2,1)}, bf16[512,512]{1,0:T(8,128)(2,1)}, u32[]{:S(2)}, u32[]{:S(2)}) collective-permute-start(bf16[512,512]{1,0:T(8,128)(2,1)} %get-tuple-element.35), channel_id=1, source_target_pairs={{13,14},{28,29},{43,44},{58,59},{73,74},{88,89},{103,104},{118,119... | collective-permute-start | bytes 1572872 | tf_op jit(solution)/shard_map/ppermute | solution.py:90
  83.4 1.6 collective-permute-start.8
  96.8 37.7 %all-to-all-start.1 = ((bf16[16,64,512]{2,1,0:T(8,128)(2,1)}), bf16[16,64,512]{2,1,0:T(8,128)(2,1)}, u32[]{:S(2)}, u32[]{:S(2)}) async-start(bf16[16,64,512]{2,1,0:T(8,128)(2,1)} %get-tuple-element.51), calls=%async_computation.1 | async-start | bytes 2097152 | tf_op jit(solution)/shard_map/all_to_all | solution.py:86
  112.7 5.9 %collective-permute-start.22 = (bf16[2,256,512]{2,1,0:T(8,128)(2,1)}, bf16[2,256,512]{2,1,0:T(8,128)(2,1)S(1)}, u32[]{:S(2)}, u32[]{:S(2)}) collective-permute-start(bf16[2,256,512]{2,1,0:T(8,128)(2,1)} %get-tuple-element.50), channel_id=1, source_target_pairs={{0,16},{1,17},{2,18},{3,19},{4,20},{5,21},{6,22},{7,23},{8,24},{9,... | collective-permute-start | bytes 1572872 | tf_op jit(solution)/shard_map/ppermute | solution.py:90
  112.7 9.4 %collective-permute-start.19 = (bf16[512,512]{1,0:T(8,128)(2,1)}, bf16[512,512]{1,0:T(8,128)(2,1)}, u32[]{:S(2)}, u32[]{:S(2)}) collective-permute-start(bf16[512,512]{1,0:T(8,128)(2,1)} %get-tuple-element.35), channel_id=1, source_target_pairs={{13,15},{28,30},{43,45},{58,60},{73,75},{88,90},{103,105},{118,120... | collective-permute-start | bytes 1572872 | tf_op jit(solution)/shard_map/ppermute | solution.py:90
  114.2 7.9 %collective-permute-start.18 = (bf16[512,512]{1,0:T(8,128)(2,1)}, bf16[512,512]{1,0:T(8,128)(2,1)}, u32[]{:S(2)}, u32[]{:S(2)}) collective-permute-start(bf16[512,512]{1,0:T(8,128)(2,1)} %get-tuple-element.35), channel_id=1, source_target_pairs={{13,45},{28,60},{43,75},{58,90},{73,105},{88,120},{103,135},{118,1... | collective-permute-start | bytes 1572872 | tf_op jit(solution)/shard_map/ppermute | solution.py:90
  115.6 6.5 %collective-permute-start.21 = (bf16[512,512]{1,0:T(8,128)(2,1)}, bf16[512,512]{1,0:T(8,128)(2,1)}, u32[]{:S(2)}, u32[]{:S(2)}) collective-permute-start(bf16[512,512]{1,0:T(8,128)(2,1)} %get-tuple-element.47), channel_id=1, source_target_pairs={{14,15},{29,30},{44,45},{59,60},{74,75},{89,90},{104,105},{119,120... | collective-permute-start | bytes 1572872 | tf_op jit(solution)/shard_map/ppermute | solution.py:90
  117.1 5.0 %collective-permute-start.20 = (bf16[512,512]{1,0:T(8,128)(2,1)}, bf16[512,512]{1,0:T(8,128)(2,1)}, u32[]{:S(2)}, u32[]{:S(2)}) collective-permute-start(bf16[512,512]{1,0:T(8,128)(2,1)} %get-tuple-element.47), channel_id=1, source_target_pairs={{14,30},{29,45},{44,60},{59,75},{74,90},{89,105},{104,120},{119,13... | collective-permute-start | bytes 1572872 | tf_op jit(solution)/shard_map/ppermute | solution.py:90
  120.5 36.6 %collective-permute-start.23 = (bf16[2,256,512]{2,1,0:T(8,128)(2,1)}, bf16[2,256,512]{2,1,0:T(8,128)(2,1)}, u32[]{:S(2)}, u32[]{:S(2)}) collective-permute-start(bf16[2,256,512]{2,1,0:T(8,128)(2,1)} %add.35), channel_id=1, source_target_pairs={{14,142},{30,158},{13,141},{29,157},{44,172},{60,188},{43,171},{59... | collective-permute-start | bytes 1572872 | tf_op jit(solution)/shard_map/ppermute | solution.py:90
  137.7 45.7 %all-to-all-start.2 = ((bf16[16,96,512]{2,1,0:T(8,128)(2,1)}), bf16[16,96,512]{2,1,0:T(8,128)(2,1)}, u32[]{:S(2)}, u32[]{:S(2)}) async-start(bf16[16,96,512]{2,1,0:T(8,128)(2,1)} %shard_map.70), calls=%async_computation.2 | async-start | bytes 3145728 | tf_op jit(solution)/shard_map/all_to_all | solution.py:86
  158.5 4.2 %collective-permute-start.24 = (bf16[2,256,512]{2,1,0:T(8,128)(2,1)S(1)}, bf16[2,256,512]{2,1,0:T(8,128)(2,1)S(1)}, u32[]{:S(2)}, u32[]{:S(2)}) collective-permute-start(bf16[2,256,512]{2,1,0:T(8,128)(2,1)S(1)} %add.36), channel_id=1, source_target_pairs={{142,206},{14,78},{158,94},{30,222},{141,205},{13,77},{157,93},{29... | collective-permute-start | bytes 1572872 | tf_op jit(solution)/shard_map/ppermute | solution.py:90
  159.2 2.5 %collective-permute-start.27 = (bf16[1,256,512]{2,1,0:T(8,128)(2,1)}, bf16[1,256,512]{2,1,0:T(8,128)(2,1)S(1)}, u32[]{:S(2)}, u32[]{:S(2)}) collective-permute-start(bf16[1,256,512]{2,1,0:T(8,128)(2,1)} %get-tuple-element.54), channel_id=1, source_target_pairs={{0,16},{1,17},{2,18},{3,19},{4,20},{5,21},{6,22},{7,23},{8,24},{9,... | collective-permute-start | bytes 786440 | tf_op jit(solution)/shard_map/ppermute | solution.py:90
  162.8 17.5 %collective-permute-start.25 = (bf16[2,256,512]{2,1,0:T(8,128)(2,1)S(1)}, bf16[2,256,512]{2,1,0:T(8,128)(2,1)S(1)}, u32[]{:S(2)}, u32[]{:S(2)}) collective-permute-start(bf16[2,256,512]{2,1,0:T(8,128)(2,1)S(1)} %add.37), channel_id=1, source_target_pairs={{206,238},{142,174},{78,110},{14,46},{94,62},{158,126},{222,190},{... | collective-permute-start | bytes 1572872 | tf_op jit(solution)/shard_map/ppermute | solution.py:90
  164.1 0.7 collective-permute-start.28
  164.9 16.4 %collective-permute-start.29 = (bf16[1,256,512]{2,1,0:T(8,128)(2,1)S(1)}, bf16[1,256,512]{2,1,0:T(8,128)(2,1)S(1)}, u32[]{:S(2)}, u32[]{:S(2)}) collective-permute-start(bf16[1,256,512]{2,1,0:T(8,128)(2,1)S(1)} %add.40), channel_id=1, source_target_pairs={{143,207},{15,79},{159,95},{31,223},{142,206},{14,78},{158,94},{30... | collective-permute-start | bytes 786440 | tf_op jit(solution)/shard_map/ppermute | solution.py:90
  181.2 23.4 %collective-permute-start.26 = (bf16[2,256,512]{2,1,0:T(8,128)(2,1)}, bf16[2,256,512]{2,1,0:T(8,128)(2,1)}, u32[]{:S(2)}, u32[]{:S(2)}) collective-permute-start(bf16[2,256,512]{2,1,0:T(8,128)(2,1)} %add.38.refs_6_.refs_12_), channel_id=1, source_target_pairs={{0,16},{1,17},{2,18},{3,19},{4,20},{5,21},{6,22},{7,23},{8,24},{9,... | collective-permute-start | bytes 1572872 | tf_op jit(solution)/shard_map/ppermute | solution.py:90
  182.1 19.5 %collective-permute-start.30 = (bf16[1,256,512]{2,1,0:T(8,128)(2,1)}, bf16[1,256,512]{2,1,0:T(8,128)(2,1)}, u32[]{:S(2)}, u32[]{:S(2)}) collective-permute-start(bf16[1,256,512]{2,1,0:T(8,128)(2,1)} %add.41), channel_id=1, source_target_pairs={{207,239},{143,175},{79,111},{15,47},{95,63},{159,127},{223,191},{... | collective-permute-start | bytes 786440 | tf_op jit(solution)/shard_map/ppermute | solution.py:90
  185.8 26.2 %all-to-all-start.3 = ((bf16[16,32,512]{2,1,0:T(8,128)(2,1)}), bf16[16,32,512]{2,1,0:T(8,128)(2,1)}, u32[]{:S(2)}, u32[]{:S(2)}) async-start(bf16[16,32,512]{2,1,0:T(8,128)(2,1)} %shard_map.72), calls=%async_computation.3 | async-start | bytes 1048576 | tf_op jit(solution)/shard_map/all_to_all | solution.py:86
  202.7 8.6 %copy-start = (bf16[1,256,512]{2,1,0:T(8,128)(2,1)}, bf16[1,256,512]{2,1,0:T(8,128)(2,1)S(1)}, u32[]{:S(2)}) copy-start(bf16[1,256,512]{2,1,0:T(8,128)(2,1)S(1)} %add.42.refs_3_) | copy-start | bytes 786436
  202.7 8.6 %collective-permute-start.31 = (bf16[1,256,512]{2,1,0:T(8,128)(2,1)S(1)}, bf16[1,256,512]{2,1,0:T(8,128)(2,1)S(1)}, u32[]{:S(2)}, u32[]{:S(2)}) collective-permute-start(bf16[1,256,512]{2,1,0:T(8,128)(2,1)S(1)} %add.42.refs_3_), channel_id=1, source_target_pairs={{0,16},{1,17},{2,18},{3,19},{4,20},{5,21},{6,22},{7,23},{8,24},{9,... | collective-permute-start | bytes 786440 | tf_op jit(solution)/shard_map/ppermute | solution.py:90
  212.0 1.0 copy-start.1
  213.0 0.9 copy-start.5
  (1 other events, 0.7 us)

commit v2 on v1

--- a/solution.py
+++ b/solution.py
@@ -215,19 +215,20 @@
     return jnp.concatenate([left, right], axis=1)
 
 
-def solve(source, u_pair, v_pair, scale, u_more, v_more, solved_ref):
+def doubled(u_ref, v_ref, solved_ref):
+    def once(power, carry):
+        moved = lower_times((u_ref[power, 0], u_ref[power, 1]), solved_ref[...])
+        solved_ref[...] += times_upper(moved, (v_ref[power, 0], v_ref[power, 1]))
+        return carry
+
+    lax.fori_loop(0, 2, once, 0)
+
+
+def begun(source, u_pair, v_pair, scale, solved_ref):
     right = source - lower_times(u_pair, source)
     solved_ref[...] = (right - times_upper(right, v_pair)) * scale
     moved = lower_times(u_pair, solved_ref[...])
     solved_ref[...] += times_upper(moved, v_pair)
-    u_ref, v_ref = u_more(), v_more()
-
-    def doubled(power, carry):
-        moved = lower_times((u_ref[power, 0], u_ref[power, 1]), solved_ref[...])
-        solved_ref[...] += times_upper(moved, (v_ref[power, 0], v_ref[power, 1]))
-        return carry
-
-    lax.fori_loop(0, 2, doubled, 0)
 
 
 def opening_body(shape, scalars, load, made, store):
@@ -315,15 +316,21 @@
         v_ref[power + 1, 0], v_ref[power + 1, 1] = split(times_upper(value, base))
         return carry
 
-    lax.fori_loop(0, 2, squared, 0)
+    @pl.when((at[7] >= 0) & (at[7] < FRONTS))
+    def _():
+        lax.fori_loop(0, 2, squared, 0)
+
     for power in (1, 2):
         store(0, power)
         store(1, power)
-    solve(
-        load(3)[...], (u_ref[0, 0], u_ref[0, 1]), (v_ref[0, 0], v_ref[0, 1]), scale[0],
-        lambda: u_ref.at[1:], lambda: v_ref.at[1:], solved_ref,
-    )
-    sent_ref[...] = solved_ref[...].astype(half_type)
+    source = load(3)[...]
+
+    @pl.when(at[6] > 0)
+    def _():
+        begun(source, (u_ref[0, 0], u_ref[0, 1]), (v_ref[0, 0], v_ref[0, 1]), scale[0], solved_ref)
+        doubled(u_ref.at[1:], v_ref.at[1:], solved_ref)
+        sent_ref[...] = solved_ref[...].astype(half_type)
+
     store(3)
     store(2)
 
@@ -335,20 +342,29 @@
     half = width // 2
     core, root = at[1], at[6]
     base = 3 + 5 * count
-    source = load(2)[...]
-    for n in range(count):
-        a_at, down_at, right_at, keep_at, got_at = range(3 + 5 * n, 8 + 5 * n)
-        source = source - narrow(square_of(load(a_at)), load(down_at)[...])
-        b_tile = joined(b_scr, core, load(keep_at), load(got_at))
-        source = source - narrow(load(right_at)[...], b_tile)
+    for k in range(base):
+        load(k)
     load.begin(base)
     load.begin(base + 1)
     u_ref, v_ref = load(0), load(1)
-    solve(
-        source, (u_ref[0], u_ref[1]), (v_ref[0], v_ref[1]), scale[0],
-        lambda: load(base), lambda: load(base + 1), solved_ref,
-    )
-    sent_ref[...] = solved_ref[...].astype(half_type)
+
+    @pl.when(root > 0)
+    def _():
+        source = load(2)[...]
+        for n in range(count):
+            a_at, down_at, right_at, keep_at, got_at = range(3 + 5 * n, 8 + 5 * n)
+            source = source - narrow(square_of(load(a_at)), load(down_at)[...])
+            b_tile = joined(b_scr.at[n], core, load(keep_at), load(got_at))
+            source = source - narrow(load(right_at)[...], b_tile)
+        begun(source, (u_ref[0], u_ref[1]), (v_ref[0], v_ref[1]), scale[0], solved_ref)
+
+    u_high, v_high = load(base), load(base + 1)
+
+    @pl.when(root > 0)
+    def _():
+        doubled(u_high, v_high, solved_ref)
+        sent_ref[...] = solved_ref[...].astype(half_type)
+
     store(1)
     tiles = [sent_ref] if mine_ref.shape[0] == 1 else [load(4), sent_ref]
     for n, tile in enumerate(tiles):
@@ -428,7 +444,7 @@
     @pl.when(at[7] == FRONTS)
     def _():
         for n in range(2):
-            taken_off(n, at, load, total, 4 + 6 * n, b_scr, d_scr)
+            taken_off(n, at, load, total, 4 + 6 * n, b_scr.at[n], d_scr.at[n])
 
     store(0)
 
@@ -524,6 +540,7 @@
         return opened, (slice(None), slice((2 + n) * strip, (3 + n) * strip))
 
     b_scr = pltpu.VMEM((rows, strip, width), half_type)
+    b_more = pltpu.VMEM((2, rows, strip, width), half_type)
     d_scr = pltpu.VMEM((2, half, width), half_type)
     more = [(u_list, slice(1, 3)), (v_list, slice(1, 3))]
 
@@ -533,7 +550,7 @@
         functools.partial(next_body, 1),
         [(tile, full_type), (tile, half_type), both, both, ((cols, 2 * strip, width), half_type)],
         (u_list, 0), (v_list, 0), work, a_of(0), hop_down, hop_right, (b_keep, 0), (b_got, 0), *more,
-        scalars=(at_second, scale), scratch=[b_scr], late=(8, 9),
+        scalars=(at_second, scale), scratch=[b_more], late=(8, 9),
     )
     hop_down = send(s_second, grid.moved(first + 1, 1, 0))
     hop_right = send(s_second, grid.moved(first + 1, 0, 1))
@@ -545,7 +562,7 @@
         (u_list, 0), (v_list, 0), work,
         a_of(0), far_down, far_right, (b_keep, 0), (b_got, 0),
         a_of(1), hop_down, hop_right, (b_keep, 1), (b_got, 1), *more,
-        scalars=(at_last, scale), scratch=[b_scr], late=(13, 14),
+        scalars=(at_last, scale), scratch=[b_more], late=(13, 14),
     )
     one = pltpu.SemaphoreType.DMA((1,))
     (fourth_operand,) = kernel(
@@ -578,7 +595,7 @@
         ]
     (behind,) = kernel(
         behind_body, [(tile, full_type)], work, x_first, x_second, x_third, *factors,
-        scalars=(at,), scratch=[b_scr, d_scr],
+        scalars=(at,), scratch=[b_more, pltpu.VMEM((2, 2, half, width), half_type)],
     )
     (result,) = kernel(
         behind_last_body, [(tile, full_type)],

time: 221 us -> 216 us (0.977)
  Pallas kernels: 62.5 us -> 45.5 us
  starting transfers between devices: 109 us -> 122 us
    pallas_call x10, Pallas kernels: 62.5 us -> 45.5 us  [kernel(): pl.pallas_call(run, out_shape=[PLACE(shape, kind) for shape, kind in outs...]
    all_to_all x4, starting transfers between devices: 58.7 us -> 71.2 us  [exchange(): return lax.all_to_all(array, axis, split_axis=0, concat_axis=0, tiled=True)]
  transfers between devices with their start and end apart: 36 -> 36, of which waited for: 5 -> 5; matrix products, arithmetic and copies ran while one was open for 3% -> 4% of each run, Pallas kernels for 19% -> 14%
where the time goes in v2:
time: 216 us; the launch traced here: 214 us
  starting transfers between devices  122 us (56%)
  Pallas kernels  45.5 us (21%)
  waiting for transfers between devices  32.6 us (15%)
  other arithmetic  7.36 us (3%)
  local copies, waits for them, and re-layouts  4.71 us (2%)
    all_to_all x4, starting transfers between devices, exchange(): return lax.all_to_all(array, axis, split_axis=0, concat_axis=0, tiled=True)  71.2 us
    ppermute x32, starting transfers between devices, send(): return lax.ppermute(array, ('row', 'col'), pairs)  51 us
    pallas_call x10, Pallas kernels, kernel(): pl.pallas_call(run, out_shape=[PLACE(shape, kind) for shape, kind in outs...  45.5 us
    ppermute x32, waiting for transfers between devices, send(): return lax.ppermute(array, ('row', 'col'), pairs)  32.6 us
    unnamed x26, local copies, waits for them, and re-layouts  4.46 us
    add x6, other arithmetic, spread_deep(): held = held + got  4.38 us
  transfers between devices with their start and end apart: 36, of which 5 were waited for; matrix products, arithmetic and copies ran while one was open for 4% of the time, Pallas kernels for 14%

profile of v2, /device:TPU:70, one launch (start us, length us, event | category | flops | bytes accessed | tf_op | source)
XLA Modules:
  0.0 213.8 jit_solution(2823160573759516736)
XLA Ops:
  0.1 3.9 %shard_map.64 = (bf16[16,160,512]{2,1,0:T(8,128)(2,1)}, bf16[64,512]{1,0:T(8,128)(2,1)}, bf16[128,512]{1,0:T(8,128)(2,1)}, bf16[128,512]{1,0:T(8,128)(2,1)}, bf1...) custom-call(s32[8]{0:T(128)S(1)} %stack.87.refs_0_, ...), custom_call_target="tpu_custom_call" | custom-call | tf_op jit(solution)/shard_map/pallas_call | solution.py:161
  4.1 7.6 %all-to-all-start = ((bf16[16,160,512]{2,1,0:T(8,128)(2,1)}), bf16[16,160,512]{2,1,0:T(8,128)(2,1)S(1)}, u32[]{:S(2)}, u32[]{:S(2)}) async-start(bf16[16,160,512]{2,1,0:T(8,128)(2,1)} %get-tuple-element.31), calls=%async_computation | async-start | bytes 5242880 | tf_op jit(solution)/shard_map/all_to_all | solution.py:86
  11.6 2.0 collective-permute-start.6
  13.7 1.3 collective-permute-start.5
  18.4 4.7 %collective-permute-start.10 = (bf16[128,512]{1,0:T(8,128)(2,1)}, bf16[128,512]{1,0:T(8,128)(2,1)S(1)}, u32[]{:S(2)}, u32[]{:S(2)}) collective-permute-start(bf16[128,512]{1,0:T(8,128)(2,1)} %get-tuple-element.37), channel_id=1, source_target_pairs={{11,43},{12,44},{13,45},{14,46},{15,47},{27,59},{28,60},{29,61},{3... | collective-permute-start | bytes 393224 | tf_op jit(solution)/shard_map/ppermute | solution.py:90
  23.1 6.7 %collective-permute-start.11 = (bf16[128,512]{1,0:T(8,128)(2,1)S(1)}, bf16[128,512]{1,0:T(8,128)(2,1)S(1)}, u32[]{:S(2)}, u32[]{:S(2)}) collective-permute-start(bf16[128,512]{1,0:T(8,128)(2,1)S(1)} %copy-done.12), channel_id=1, source_target_pairs={{9,73},{10,74},{11,75},{12,76},{13,77},{14,78},{15,79},{25,89},{26... | collective-permute-start | bytes 393224 | tf_op jit(solution)/shard_map/ppermute | solution.py:90
  29.9 2.5 %collective-permute-start.12 = (bf16[128,512]{1,0:T(8,128)(2,1)S(1)}, bf16[128,512]{1,0:T(8,128)(2,1)S(1)}, u32[]{:S(2)}, u32[]{:S(2)}) collective-permute-start(bf16[128,512]{1,0:T(8,128)(2,1)S(1)} %copy-done.11), channel_id=1, source_target_pairs={{7,103},{8,104},{9,105},{10,106},{11,107},{12,108},{13,109},{14,11... | collective-permute-start | bytes 393224 | tf_op jit(solution)/shard_map/ppermute | solution.py:90
  32.4 2.6 %shard_map.65.refs_2_ = bf16[8,64,512]{2,1,0:T(8,128)(2,1)} custom-call(s32[8]{0:T(128)S(1)} %stack.87.refs_0_, bf16[64,512]{1,0:T(8,128)(2,1)} %get-tuple-element.30.refs_1_, bf16[64,512]{1,0:T(8,128)(2,1)S(1)} %collective-permute-done.refs_2_, bf16[64,512]{1,0:T(8,128)(2,1)S(1)} %collective-permute-done.1.refs_3_, ...), custom_call_target="tpu_custom_call" | custom-call | tf_op jit(solution)/shard_map/pallas_call | solution.py:161
  35.1 5.7 %collective-permute-start.13 = (bf16[128,512]{1,0:T(8,128)(2,1)S(1)}, bf16[128,512]{1,0:T(8,128)(2,1)S(1)}, u32[]{:S(2)}, u32[]{:S(2)}) collective-permute-start(bf16[128,512]{1,0:T(8,128)(2,1)S(1)} %copy-done.10), channel_id=1, source_target_pairs={{5,133},{6,134},{7,135},{8,136},{9,137},{10,138},{11,139},{12,140}... | collective-permute-start | bytes 393224 | tf_op jit(solution)/shard_map/ppermute | solution.py:90
  40.8 3.2 %collective-permute-start.14 = (bf16[128,512]{1,0:T(8,128)(2,1)S(1)}, bf16[128,512]{1,0:T(8,128)(2,1)S(1)}, u32[]{:S(2)}, u32[]{:S(2)}) collective-permute-start(bf16[128,512]{1,0:T(8,128)(2,1)S(1)} %copy-done.9), channel_id=1, source_target_pairs={{3,163},{4,164},{5,165},{6,166},{7,167},{8,168},{9,169},{10,170},{... | collective-permute-start | bytes 393224 | tf_op jit(solution)/shard_map/ppermute | solution.py:90
  44.0 3.3 %collective-permute-done.11.refs_3_ = bf16[128,512]{1,0:T(8,128)(2,1)S(1)} collective-permute-done((bf16[128,512]{1,0:T(8,128)(2,1)S(1)}, bf16[128,512]{1,0:T(8,128)(2,1)S(1)}, u32[]{:S(2)}, u32[]{:S(2)}) %collective-permute-start.11) | collective-permute-done | bytes 131104 | tf_op jit(solution)/shard_map/ppermute | solution.py:90
  47.4 1.3 collective-permute-start.15
  48.7 1.9 collective-permute-start.16
  50.6 7.6 %collective-permute-done.14.refs_6_ = bf16[128,512]{1,0:T(8,128)(2,1)S(1)} collective-permute-done((bf16[128,512]{1,0:T(8,128)(2,1)S(1)}, bf16[128,512]{1,0:T(8,128)(2,1)S(1)}, u32[]{:S(2)}, u32[]{:S(2)}) %collective-permute-start.14) | collective-permute-done | bytes 131104 | tf_op jit(solution)/shard_map/ppermute | solution.py:90
  58.2 5.7 %collective-permute-done.15.refs_7_ = bf16[128,512]{1,0:T(8,128)(2,1)S(1)} collective-permute-done((bf16[128,512]{1,0:T(8,128)(2,1)S(1)}, bf16[128,512]{1,0:T(8,128)(2,1)S(1)}, u32[]{:S(2)}, u32[]{:S(2)}) %collective-permute-start.15) | collective-permute-done | bytes 131104 | tf_op jit(solution)/shard_map/ppermute | solution.py:90
  63.9 3.3 %shard_map.67 = (bf16[3,8,32,512]{3,2,1,0:T(8,128)(2,1)}, bf16[3,8,32,512]{3,2,1,0:T(8,128)(2,1)}) custom-call(s32[8]{0:T(128)S(1)} %stack.87.refs_0_, bf16[128,512]{1,0:T(8,128)(2,1)} %get-tuple-element.36.refs_1_, bf16[128,512]{1,0:T(8,128)(2,1)S(1)} %collective-permute-done.10.refs_2_, bf16[128,512]{1,0:T(8,128)(2,1)S(1)} %collective-permute-done.11.refs_3_, ...), custom_call_target="tpu_custom_call" | custom-call | tf_op jit(solution)/shard_map/pallas_call | solution.py:161
  68.8 1.0 copy-done.3
  69.9 5.1 %shard_map.66 = (bf16[3,2,512,512]{3,2,1,0:T(8,128)(2,1)}, bf16[3,2,512,512]{3,2,1,0:T(8,128)(2,1)}, f32[512,512]{1,0:T(8,128)}, bf16[512,512]{1,0:T(8,128)(2,1)}) custom-call(s32[8]{0:T(128)S(1)} %stack.87.refs_0_, f32[1]{0:T(128)S(6)} %div.14.refs_1_, bf16[8,64,512]{2,1,0:T(8,128)(2,1)} %shard_map.65.refs_2_, bf16[8,64,512]{2,1,0:T(8,128)(2,1)S(1)} %copy-done.3, ...), custom_call_target="tpu_custom_call" | custom-call | tf_op jit(solution)/shard_map/pallas_call | solution.py:161
  75.0 1.5 collective-permute-start.9
  76.5 1.5 collective-permute-start.8
  78.1 7.1 %shard_map.68 = (f32[512,512]{1,0:T(8,128)}, bf16[512,512]{1,0:T(8,128)(2,1)}, bf16[2,256,512]{2,1,0:T(8,128)(2,1)}, bf16[2,256,512]{2,1,0:T(8,128)(2,1)}, bf16[16,64,512]{2,1,0:T(8,128)(2,1)}) custom-call(s32[8]{0:T(128)S(1)} %stack.91.refs_0_, f32[1]{0:T(128)S(6)} %div.14.refs_1_, bf16[3,2,512,512]{3,2,1,0:T(8,128)(2,1)} %get-tuple-element.33.refs_2_.refs_10_.refs_15_, ...), custom_call_target="tpu_custom_call" | custom-call | tf_op jit(solution)/shard_map/pallas_call | solution.py:161
  85.2 26.6 %all-to-all-start.1 = ((bf16[16,64,512]{2,1,0:T(8,128)(2,1)}), bf16[16,64,512]{2,1,0:T(8,128)(2,1)}, u32[]{:S(2)}, u32[]{:S(2)}) async-start(bf16[16,64,512]{2,1,0:T(8,128)(2,1)} %get-tuple-element.51), calls=%async_computation.1 | async-start | bytes 2097152 | tf_op jit(solution)/shard_map/all_to_all | solution.py:86
  111.8 1.5 collective-permute-start.19
  113.3 1.5 collective-permute-start.18
  114.7 1.5 collective-permute-start.21
  116.2 1.4 collective-permute-start.20
  117.6 2.0 add.35
  119.6 1.5 collective-permute-start.23
  121.2 7.1 %shard_map.69 = (f32[512,512]{1,0:T(8,128)}, bf16[512,512]{1,0:T(8,128)(2,1)}, bf16[1,256,512]{2,1,0:T(8,128)(2,1)}, bf16[1,256,512]{2,1,0:T(8,128)(2,1)}) custom-call(s32[8]{0:T(128)S(1)} %stack.95.refs_0_, f32[1]{0:T(128)S(6)} %div.14.refs_1_, bf16[3,2,512,512]{3,2,1,0:T(8,128)(2,1)} %get-tuple-element.33.refs_2_.refs_10_.refs_15_, ...), custom_call_target="tpu_custom_call" | custom-call | tf_op jit(solution)/shard_map/pallas_call | solution.py:161
  128.3 3.1 %shard_map.70 = bf16[16,96,512]{2,1,0:T(8,128)(2,1)} custom-call(s32[8]{0:T(128)S(1)} %stack.91.refs_0_, bf16[16,64,512]{2,1,0:T(8,128)(2,1)} %all-to-all-done.1.refs_1_, bf16[512,512]{1,0:T(8,128)(2,1)} %get-tuple-element.52.refs_2_), custom_call_target="tpu_custom_call" | custom-call | tf_op jit(solution)/shard_map/pallas_call | solution.py:161
  131.4 21.1 %all-to-all-start.2 = ((bf16[16,96,512]{2,1,0:T(8,128)(2,1)}), bf16[16,96,512]{2,1,0:T(8,128)(2,1)}, u32[]{:S(2)}, u32[]{:S(2)}) async-start(bf16[16,96,512]{2,1,0:T(8,128)(2,1)} %shard_map.70), calls=%async_computation.2 | async-start | bytes 3145728 | tf_op jit(solution)/shard_map/all_to_all | solution.py:86
  152.5 1.3 add.36
  154.6 1.2 collective-permute-start.27
  155.8 1.4 collective-permute-done.27
  157.2 1.0 add.39
  158.3 1.3 collective-permute-start.25
  161.1 14.5 %collective-permute-done.25 = bf16[2,256,512]{2,1,0:T(8,128)(2,1)S(1)} collective-permute-done((bf16[2,256,512]{2,1,0:T(8,128)(2,1)S(1)}, bf16[2,256,512]{2,1,0:T(8,128)(2,1)S(1)}, u32[]{:S(2)}, u32[]{:S(2)}) %collective-permute-start.25) | collective-permute-done | bytes 524320 | tf_op jit(solution)/shard_map/ppermute | solution.py:90
  175.6 0.9 add.38.refs_6_.refs_12_
  176.5 0.8 add.41
  177.4 1.3 collective-permute-start.30
  178.6 2.4 %shard_map.72 = bf16[16,32,512]{2,1,0:T(8,128)(2,1)} custom-call(s32[8]{0:T(128)S(1)} %stack.95.refs_0_, bf16[16,96,512]{2,1,0:T(8,128)(2,1)} %all-to-all-done.2.refs_8_.refs_14_.refs_1_), custom_call_target="tpu_custom_call" | custom-call | tf_op jit(solution)/shard_map/pallas_call | solution.py:161
  181.0 16.0 %all-to-all-start.3 = ((bf16[16,32,512]{2,1,0:T(8,128)(2,1)}), bf16[16,32,512]{2,1,0:T(8,128)(2,1)}, u32[]{:S(2)}, u32[]{:S(2)}) async-start(bf16[16,32,512]{2,1,0:T(8,128)(2,1)} %shard_map.72), calls=%async_computation.3 | async-start | bytes 1048576 | tf_op jit(solution)/shard_map/all_to_all | solution.py:86
  197.0 1.1 add.42.refs_3_
  198.1 2.0 collective-permute-start.31
  200.1 6.7 %shard_map.71.refs_1_ = f32[512,512]{1,0:T(8,128)} custom-call(s32[8]{0:T(128)S(1)} %stack.87.refs_0_, f32[512,512]{1,0:T(8,128)} %refs_1_.3, f32[512,512]{1,0:T(8,128)} %get-tuple-element.32.refs_2_, f32[512,512]{1,0:T(8,128)} %get-tuple-element.46.refs_3_, f32[512,512]{1,0:T(8,128)} %get-tuple-element.48.refs_4_, ...), custom_call_target="tpu_custom_call" | custom-call | tf_op jit(solution)/shard_map/pallas_call | solution.py:161
  207.6 0.9 copy-done.1
  208.5 0.9 copy-done.5
  209.5 4.2 %shard_map.73 = f32[512,512]{1,0:T(8,128)} custom-call(s32[8]{0:T(128)S(1)} %stack.87.refs_0_, f32[512,512]{1,0:T(8,128)} %shard_map.71.refs_1_, bf16[16,160,512]{2,1,0:T(8,128)(2,1)S(1)} %all-to-all-done.refs_4_.refs_5_.refs_10_.refs_11_.refs_2_, bf16[1,256,512]{2,1,0:T(8,128)(2,1)S(1)} %copy-done.1, bf16[1,256,512]{2,1,0:T(8,128)(2,1)S(1)} %copy-done.5, ...), custom_call_target="tpu_custom_call" | custom-call | tf_op jit(solution)/shard_map/pallas_call | solution.py:161
  (71 shorter events, 7.6 us)
Async XLA Ops:
  4.0 7.6 %copy-start.6 = (bf16[64,512]{1,0:T(8,128)(2,1)S(1)}, bf16[64,512]{1,0:T(8,128)(2,1)}, u32[]{:S(2)}) copy-start(bf16[64,512]{1,0:T(8,128)(2,1)} %get-tuple-element.30.refs_1_) | copy-start | bytes 196612
  4.0 19.1 %copy-start.12 = (bf16[128,512]{1,0:T(8,128)(2,1)S(1)}, bf16[128,512]{1,0:T(8,128)(2,1)}, u32[]{:S(2)}) copy-start(bf16[128,512]{1,0:T(8,128)(2,1)} %get-tuple-element.38) | copy-start | bytes 393220
  4.0 25.9 %copy-start.11 = (bf16[128,512]{1,0:T(8,128)(2,1)S(1)}, bf16[128,512]{1,0:T(8,128)(2,1)}, u32[]{:S(2)}) copy-start(bf16[128,512]{1,0:T(8,128)(2,1)} %get-tuple-element.39) | copy-start | bytes 393220
  4.0 31.1 %copy-start.10 = (bf16[128,512]{1,0:T(8,128)(2,1)S(1)}, bf16[128,512]{1,0:T(8,128)(2,1)}, u32[]{:S(2)}) copy-start(bf16[128,512]{1,0:T(8,128)(2,1)} %get-tuple-element.40) | copy-start | bytes 393220
  4.0 36.8 %copy-start.9 = (bf16[128,512]{1,0:T(8,128)(2,1)S(1)}, bf16[128,512]{1,0:T(8,128)(2,1)}, u32[]{:S(2)}) copy-start(bf16[128,512]{1,0:T(8,128)(2,1)} %get-tuple-element.41) | copy-start | bytes 393220
  4.0 43.3 %copy-start.8 = (bf16[128,512]{1,0:T(8,128)(2,1)S(1)}, bf16[128,512]{1,0:T(8,128)(2,1)}, u32[]{:S(2)}) copy-start(bf16[128,512]{1,0:T(8,128)(2,1)} %get-tuple-element.42) | copy-start | bytes 393220
  4.0 44.6 %copy-start.7 = (bf16[128,512]{1,0:T(8,128)(2,1)S(1)}, bf16[128,512]{1,0:T(8,128)(2,1)}, u32[]{:S(2)}) copy-start(bf16[128,512]{1,0:T(8,128)(2,1)} %get-tuple-element.43) | copy-start | bytes 393220
  4.1 64.8 %all-to-all-start = ((bf16[16,160,512]{2,1,0:T(8,128)(2,1)}), bf16[16,160,512]{2,1,0:T(8,128)(2,1)S(1)}, u32[]{:S(2)}, u32[]{:S(2)}) async-start(bf16[16,160,512]{2,1,0:T(8,128)(2,1)} %get-tuple-element.31), calls=%async_computation | async-start | bytes 5242880 | tf_op jit(solution)/shard_map/all_to_all | solution.py:86
  11.6 5.3 %collective-permute-start.6 = (bf16[64,512]{1,0:T(8,128)(2,1)S(1)}, bf16[64,512]{1,0:T(8,128)(2,1)S(1)}, u32[]{:S(2)}, u32[]{:S(2)}) collective-permute-start(bf16[64,512]{1,0:T(8,128)(2,1)S(1)} %copy-done.6), channel_id=1, source_target_pairs={{0,224},{1,225},{16,240},{17,241},{44,12},{45,13},{46,14},{47,15},... | collective-permute-start | bytes 196616 | tf_op jit(solution)/shard_map/ppermute | solution.py:90
  13.7 4.0 %collective-permute-start.5 = (bf16[64,512]{1,0:T(8,128)(2,1)S(1)}, bf16[64,512]{1,0:T(8,128)(2,1)S(1)}, u32[]{:S(2)}, u32[]{:S(2)}) collective-permute-start(bf16[64,512]{1,0:T(8,128)(2,1)S(1)} %copy-done.6), channel_id=1, source_target_pairs={{0,192},{1,193},{2,194},{3,195},{16,208},{17,209},{18,210},{19,211... | collective-permute-start | bytes 196616 | tf_op jit(solution)/shard_map/ppermute | solution.py:90
  15.0 3.4 %collective-permute-start.4 = (bf16[64,512]{1,0:T(8,128)(2,1)S(1)}, bf16[64,512]{1,0:T(8,128)(2,1)S(1)}, u32[]{:S(2)}, u32[]{:S(2)}) collective-permute-start(bf16[64,512]{1,0:T(8,128)(2,1)S(1)} %copy-done.6), channel_id=1, source_target_pairs={{2,162},{3,163},{4,164},{5,165},{18,178},{19,179},{20,180},{21,181... | collective-permute-start | bytes 196616 | tf_op jit(solution)/shard_map/ppermute | solution.py:90
  15.6 7.5 %collective-permute-start.3 = (bf16[64,512]{1,0:T(8,128)(2,1)S(1)}, bf16[64,512]{1,0:T(8,128)(2,1)S(1)}, u32[]{:S(2)}, u32[]{:S(2)}) collective-permute-start(bf16[64,512]{1,0:T(8,128)(2,1)S(1)} %copy-done.6), channel_id=1, source_target_pairs={{4,132},{5,133},{6,134},{7,135},{20,148},{21,149},{22,150},{23,151... | collective-permute-start | bytes 196616 | tf_op jit(solution)/shard_map/ppermute | solution.py:90
  16.3 13.5 %collective-permute-start.2 = (bf16[64,512]{1,0:T(8,128)(2,1)S(1)}, bf16[64,512]{1,0:T(8,128)(2,1)S(1)}, u32[]{:S(2)}, u32[]{:S(2)}) collective-permute-start(bf16[64,512]{1,0:T(8,128)(2,1)S(1)} %copy-done.6), channel_id=1, source_target_pairs={{6,102},{7,103},{8,104},{9,105},{22,118},{23,119},{24,120},{25,121... | collective-permute-start | bytes 196616 | tf_op jit(solution)/shard_map/ppermute | solution.py:90
  17.0 15.4 %collective-permute-start.1 = (bf16[64,512]{1,0:T(8,128)(2,1)S(1)}, bf16[64,512]{1,0:T(8,128)(2,1)S(1)}, u32[]{:S(2)}, u32[]{:S(2)}) collective-permute-start(bf16[64,512]{1,0:T(8,128)(2,1)S(1)} %copy-done.6), channel_id=1, source_target_pairs={{8,72},{9,73},{10,74},{11,75},{24,88},{25,89},{26,90},{27,91},{38,... | collective-permute-start | bytes 196616 | tf_op jit(solution)/shard_map/ppermute | solution.py:90
  17.7 14.8 %collective-permute-start = (bf16[64,512]{1,0:T(8,128)(2,1)S(1)}, bf16[64,512]{1,0:T(8,128)(2,1)S(1)}, u32[]{:S(2)}, u32[]{:S(2)}) collective-permute-start(bf16[64,512]{1,0:T(8,128)(2,1)S(1)} %copy-done.6), channel_id=1, source_target_pairs={{10,42},{11,43},{12,44},{13,45},{26,58},{27,59},{28,60},{29,61},{4... | collective-permute-start | bytes 196616 | tf_op jit(solution)/shard_map/ppermute | solution.py:90
  18.4 22.5 %collective-permute-start.10 = (bf16[128,512]{1,0:T(8,128)(2,1)}, bf16[128,512]{1,0:T(8,128)(2,1)S(1)}, u32[]{:S(2)}, u32[]{:S(2)}) collective-permute-start(bf16[128,512]{1,0:T(8,128)(2,1)} %get-tuple-element.37), channel_id=1, source_target_pairs={{11,43},{12,44},{13,45},{14,46},{15,47},{27,59},{28,60},{29,61},{3... | collective-permute-start | bytes 393224 | tf_op jit(solution)/shard_map/ppermute | solution.py:90
  23.1 24.2 %collective-permute-start.11 = (bf16[128,512]{1,0:T(8,128)(2,1)S(1)}, bf16[128,512]{1,0:T(8,128)(2,1)S(1)}, u32[]{:S(2)}, u32[]{:S(2)}) collective-permute-start(bf16[128,512]{1,0:T(8,128)(2,1)S(1)} %copy-done.12), channel_id=1, source_target_pairs={{9,73},{10,74},{11,75},{12,76},{13,77},{14,78},{15,79},{25,89},{26... | collective-permute-start | bytes 393224 | tf_op jit(solution)/shard_map/ppermute | solution.py:90
  29.9 18.8 %collective-permute-start.12 = (bf16[128,512]{1,0:T(8,128)(2,1)S(1)}, bf16[128,512]{1,0:T(8,128)(2,1)S(1)}, u32[]{:S(2)}, u32[]{:S(2)}) collective-permute-start(bf16[128,512]{1,0:T(8,128)(2,1)S(1)} %copy-done.11), channel_id=1, source_target_pairs={{7,103},{8,104},{9,105},{10,106},{11,107},{12,108},{13,109},{14,11... | collective-permute-start | bytes 393224 | tf_op jit(solution)/shard_map/ppermute | solution.py:90
  35.0 33.0 %collective-permute-start.7 = (bf16[8,64,512]{2,1,0:T(8,128)(2,1)}, bf16[8,64,512]{2,1,0:T(8,128)(2,1)S(1)}, u32[]{:S(2)}, u32[]{:S(2)}) collective-permute-start(bf16[8,64,512]{2,1,0:T(8,128)(2,1)} %shard_map.65.refs_2_), channel_id=1, source_target_pairs={{0,16},{1,17},{2,18},{3,19},{4,20},{5,21},{6,22},{7,23},{8,24},{9,... | collective-permute-start | bytes 1572872 | tf_op jit(solution)/shard_map/ppermute | solution.py:90
  35.1 15.5 %collective-permute-start.13 = (bf16[128,512]{1,0:T(8,128)(2,1)S(1)}, bf16[128,512]{1,0:T(8,128)(2,1)S(1)}, u32[]{:S(2)}, u32[]{:S(2)}) collective-permute-start(bf16[128,512]{1,0:T(8,128)(2,1)S(1)} %copy-done.10), channel_id=1, source_target_pairs={{5,133},{6,134},{7,135},{8,136},{9,137},{10,138},{11,139},{12,140}... | collective-permute-start | bytes 393224 | tf_op jit(solution)/shard_map/ppermute | solution.py:90
  40.8 17.4 %collective-permute-start.14 = (bf16[128,512]{1,0:T(8,128)(2,1)S(1)}, bf16[128,512]{1,0:T(8,128)(2,1)S(1)}, u32[]{:S(2)}, u32[]{:S(2)}) collective-permute-start(bf16[128,512]{1,0:T(8,128)(2,1)S(1)} %copy-done.9), channel_id=1, source_target_pairs={{3,163},{4,164},{5,165},{6,166},{7,167},{8,168},{9,169},{10,170},{... | collective-permute-start | bytes 393224 | tf_op jit(solution)/shard_map/ppermute | solution.py:90
  47.4 16.6 %collective-permute-start.15 = (bf16[128,512]{1,0:T(8,128)(2,1)S(1)}, bf16[128,512]{1,0:T(8,128)(2,1)S(1)}, u32[]{:S(2)}, u32[]{:S(2)}) collective-permute-start(bf16[128,512]{1,0:T(8,128)(2,1)S(1)} %copy-done.8), channel_id=1, source_target_pairs={{1,193},{2,194},{3,195},{4,196},{5,197},{6,198},{7,199},{8,200},{9... | collective-permute-start | bytes 393224 | tf_op jit(solution)/shard_map/ppermute | solution.py:90
  48.7 15.3 %collective-permute-start.16 = (bf16[128,512]{1,0:T(8,128)(2,1)S(1)}, bf16[128,512]{1,0:T(8,128)(2,1)S(1)}, u32[]{:S(2)}, u32[]{:S(2)}) collective-permute-start(bf16[128,512]{1,0:T(8,128)(2,1)S(1)} %copy-done.7), channel_id=1, source_target_pairs={{0,224},{1,225},{2,226},{3,227},{4,228},{5,229},{6,230},{7,231},{8... | collective-permute-start | bytes 393224 | tf_op jit(solution)/shard_map/ppermute | solution.py:90
  67.2 10.8 %collective-permute-start.17 = (bf16[3,8,32,512]{3,2,1,0:T(8,128)(2,1)}, bf16[3,8,32,512]{3,2,1,0:T(8,128)(2,1)S(1)}, u32[]{:S(2)}, u32[]{:S(2)}) collective-permute-start(bf16[3,8,32,512]{3,2,1,0:T(8,128)(2,1)} %get-tuple-element.45), channel_id=1, source_target_pairs={{0,16},{1,17},{2,18},{3,19},{4,20},{5,21},{6,22},{7,23},{8,24},{9,... | collective-permute-start | bytes 2359304 | tf_op jit(solution)/shard_map/ppermute | solution.py:90
  68.0 0.8 copy-start.2
  68.8 1.0 copy-start.3
  75.0 3.0 %collective-permute-start.9 = (bf16[512,512]{1,0:T(8,128)(2,1)}, bf16[512,512]{1,0:T(8,128)(2,1)}, u32[]{:S(2)}, u32[]{:S(2)}) collective-permute-start(bf16[512,512]{1,0:T(8,128)(2,1)} %get-tuple-element.35), channel_id=1, source_target_pairs={{13,14},{28,29},{43,44},{58,59},{73,74},{88,89},{103,104},{118,119... | collective-permute-start | bytes 1572872 | tf_op jit(solution)/shard_map/ppermute | solution.py:90
  76.5 1.6 collective-permute-start.8
  85.2 43.1 %all-to-all-start.1 = ((bf16[16,64,512]{2,1,0:T(8,128)(2,1)}), bf16[16,64,512]{2,1,0:T(8,128)(2,1)}, u32[]{:S(2)}, u32[]{:S(2)}) async-start(bf16[16,64,512]{2,1,0:T(8,128)(2,1)} %get-tuple-element.51), calls=%async_computation.1 | async-start | bytes 2097152 | tf_op jit(solution)/shard_map/all_to_all | solution.py:86
  111.8 5.9 %collective-permute-start.22 = (bf16[2,256,512]{2,1,0:T(8,128)(2,1)}, bf16[2,256,512]{2,1,0:T(8,128)(2,1)S(1)}, u32[]{:S(2)}, u32[]{:S(2)}) collective-permute-start(bf16[2,256,512]{2,1,0:T(8,128)(2,1)} %get-tuple-element.50), channel_id=1, source_target_pairs={{0,16},{1,17},{2,18},{3,19},{4,20},{5,21},{6,22},{7,23},{8,24},{9,... | collective-permute-start | bytes 1572872 | tf_op jit(solution)/shard_map/ppermute | solution.py:90
  111.8 9.4 %collective-permute-start.19 = (bf16[512,512]{1,0:T(8,128)(2,1)}, bf16[512,512]{1,0:T(8,128)(2,1)}, u32[]{:S(2)}, u32[]{:S(2)}) collective-permute-start(bf16[512,512]{1,0:T(8,128)(2,1)} %get-tuple-element.35), channel_id=1, source_target_pairs={{13,15},{28,30},{43,45},{58,60},{73,75},{88,90},{103,105},{118,120... | collective-permute-start | bytes 1572872 | tf_op jit(solution)/shard_map/ppermute | solution.py:90
  113.3 7.9 %collective-permute-start.18 = (bf16[512,512]{1,0:T(8,128)(2,1)}, bf16[512,512]{1,0:T(8,128)(2,1)}, u32[]{:S(2)}, u32[]{:S(2)}) collective-permute-start(bf16[512,512]{1,0:T(8,128)(2,1)} %get-tuple-element.35), channel_id=1, source_target_pairs={{13,45},{28,60},{43,75},{58,90},{73,105},{88,120},{103,135},{118,1... | collective-permute-start | bytes 1572872 | tf_op jit(solution)/shard_map/ppermute | solution.py:90
  114.7 6.5 %collective-permute-start.21 = (bf16[512,512]{1,0:T(8,128)(2,1)}, bf16[512,512]{1,0:T(8,128)(2,1)}, u32[]{:S(2)}, u32[]{:S(2)}) collective-permute-start(bf16[512,512]{1,0:T(8,128)(2,1)} %get-tuple-element.47), channel_id=1, source_target_pairs={{14,15},{29,30},{44,45},{59,60},{74,75},{89,90},{104,105},{119,120... | collective-permute-start | bytes 1572872 | tf_op jit(solution)/shard_map/ppermute | solution.py:90
  116.2 5.0 %collective-permute-start.20 = (bf16[512,512]{1,0:T(8,128)(2,1)}, bf16[512,512]{1,0:T(8,128)(2,1)}, u32[]{:S(2)}, u32[]{:S(2)}) collective-permute-start(bf16[512,512]{1,0:T(8,128)(2,1)} %get-tuple-element.47), channel_id=1, source_target_pairs={{14,30},{29,45},{44,60},{59,75},{74,90},{89,105},{104,120},{119,13... | collective-permute-start | bytes 1572872 | tf_op jit(solution)/shard_map/ppermute | solution.py:90
  119.6 32.9 %collective-permute-start.23 = (bf16[2,256,512]{2,1,0:T(8,128)(2,1)}, bf16[2,256,512]{2,1,0:T(8,128)(2,1)}, u32[]{:S(2)}, u32[]{:S(2)}) collective-permute-start(bf16[2,256,512]{2,1,0:T(8,128)(2,1)} %add.35), channel_id=1, source_target_pairs={{14,142},{30,158},{13,141},{29,157},{44,172},{60,188},{43,171},{59... | collective-permute-start | bytes 1572872 | tf_op jit(solution)/shard_map/ppermute | solution.py:90
  131.4 47.2 %all-to-all-start.2 = ((bf16[16,96,512]{2,1,0:T(8,128)(2,1)}), bf16[16,96,512]{2,1,0:T(8,128)(2,1)}, u32[]{:S(2)}, u32[]{:S(2)}) async-start(bf16[16,96,512]{2,1,0:T(8,128)(2,1)} %shard_map.70), calls=%async_computation.2 | async-start | bytes 3145728 | tf_op jit(solution)/shard_map/all_to_all | solution.py:86
  153.9 4.3 %collective-permute-start.24 = (bf16[2,256,512]{2,1,0:T(8,128)(2,1)S(1)}, bf16[2,256,512]{2,1,0:T(8,128)(2,1)S(1)}, u32[]{:S(2)}, u32[]{:S(2)}) collective-permute-start(bf16[2,256,512]{2,1,0:T(8,128)(2,1)S(1)} %add.36), channel_id=1, source_target_pairs={{142,206},{14,78},{158,94},{30,222},{141,205},{13,77},{157,93},{29... | collective-permute-start | bytes 1572872 | tf_op jit(solution)/shard_map/ppermute | solution.py:90
  154.6 2.6 %collective-permute-start.27 = (bf16[1,256,512]{2,1,0:T(8,128)(2,1)}, bf16[1,256,512]{2,1,0:T(8,128)(2,1)S(1)}, u32[]{:S(2)}, u32[]{:S(2)}) collective-permute-start(bf16[1,256,512]{2,1,0:T(8,128)(2,1)} %get-tuple-element.54), channel_id=1, source_target_pairs={{0,16},{1,17},{2,18},{3,19},{4,20},{5,21},{6,22},{7,23},{8,24},{9,... | collective-permute-start | bytes 786440 | tf_op jit(solution)/shard_map/ppermute | solution.py:90
  158.3 17.3 %collective-permute-start.25 = (bf16[2,256,512]{2,1,0:T(8,128)(2,1)S(1)}, bf16[2,256,512]{2,1,0:T(8,128)(2,1)S(1)}, u32[]{:S(2)}, u32[]{:S(2)}) collective-permute-start(bf16[2,256,512]{2,1,0:T(8,128)(2,1)S(1)} %add.37), channel_id=1, source_target_pairs={{206,238},{142,174},{78,110},{14,46},{94,62},{158,126},{222,190},{... | collective-permute-start | bytes 1572872 | tf_op jit(solution)/shard_map/ppermute | solution.py:90
  159.6 0.7 collective-permute-start.28
  160.4 16.1 %collective-permute-start.29 = (bf16[1,256,512]{2,1,0:T(8,128)(2,1)S(1)}, bf16[1,256,512]{2,1,0:T(8,128)(2,1)S(1)}, u32[]{:S(2)}, u32[]{:S(2)}) collective-permute-start(bf16[1,256,512]{2,1,0:T(8,128)(2,1)S(1)} %add.40), channel_id=1, source_target_pairs={{143,207},{15,79},{159,95},{31,223},{142,206},{14,78},{158,94},{30... | collective-permute-start | bytes 786440 | tf_op jit(solution)/shard_map/ppermute | solution.py:90
  176.5 23.6 %collective-permute-start.26 = (bf16[2,256,512]{2,1,0:T(8,128)(2,1)}, bf16[2,256,512]{2,1,0:T(8,128)(2,1)}, u32[]{:S(2)}, u32[]{:S(2)}) collective-permute-start(bf16[2,256,512]{2,1,0:T(8,128)(2,1)} %add.38.refs_6_.refs_12_), channel_id=1, source_target_pairs={{0,16},{1,17},{2,18},{3,19},{4,20},{5,21},{6,22},{7,23},{8,24},{9,... | collective-permute-start | bytes 1572872 | tf_op jit(solution)/shard_map/ppermute | solution.py:90
  177.4 19.6 %collective-permute-start.30 = (bf16[1,256,512]{2,1,0:T(8,128)(2,1)}, bf16[1,256,512]{2,1,0:T(8,128)(2,1)}, u32[]{:S(2)}, u32[]{:S(2)}) collective-permute-start(bf16[1,256,512]{2,1,0:T(8,128)(2,1)} %add.41), channel_id=1, source_target_pairs={{207,239},{143,175},{79,111},{15,47},{95,63},{159,127},{223,191},{... | collective-permute-start | bytes 786440 | tf_op jit(solution)/shard_map/ppermute | solution.py:90
  181.0 26.5 %all-to-all-start.3 = ((bf16[16,32,512]{2,1,0:T(8,128)(2,1)}), bf16[16,32,512]{2,1,0:T(8,128)(2,1)}, u32[]{:S(2)}, u32[]{:S(2)}) async-start(bf16[16,32,512]{2,1,0:T(8,128)(2,1)} %shard_map.72), calls=%async_computation.3 | async-start | bytes 1048576 | tf_op jit(solution)/shard_map/all_to_all | solution.py:86
  198.1 8.8 %copy-start = (bf16[1,256,512]{2,1,0:T(8,128)(2,1)}, bf16[1,256,512]{2,1,0:T(8,128)(2,1)S(1)}, u32[]{:S(2)}) copy-start(bf16[1,256,512]{2,1,0:T(8,128)(2,1)S(1)} %add.42.refs_3_) | copy-start | bytes 786436
  198.1 8.8 %collective-permute-start.31 = (bf16[1,256,512]{2,1,0:T(8,128)(2,1)S(1)}, bf16[1,256,512]{2,1,0:T(8,128)(2,1)S(1)}, u32[]{:S(2)}, u32[]{:S(2)}) collective-permute-start(bf16[1,256,512]{2,1,0:T(8,128)(2,1)S(1)} %add.42.refs_3_), channel_id=1, source_target_pairs={{0,16},{1,17},{2,18},{3,19},{4,20},{5,21},{6,22},{7,23},{8,24},{9,... | collective-permute-start | bytes 786440 | tf_op jit(solution)/shard_map/ppermute | solution.py:90
  207.6 1.0 copy-start.1
  208.5 0.9 copy-start.5
  (1 other events, 0.7 us)

commit v3 on v2

--- a/solution.py
+++ b/solution.py
@@ -99,7 +99,7 @@
     return array
 
 
-def kernel(body, outs, *operands, scalars=(), scratch=(), late=()):
+def kernel(body, outs, *operands, scalars=(), scratch=(), late=(), when=None, other=None):
     operands = [one if isinstance(one, tuple) else (one, None) for one in operands]
     parts = [
         (8, 128)
@@ -118,45 +118,55 @@
 
         given, inputs, results = take(len(scalars)), take(many), take(len(outs))
         held, made, (arrival, departure) = take(many), take(len(outs)), take(2)
-        copies = []
-        begun, waited, started = set(), set(), []
-        for k, (one, part) in enumerate(operands):
-            source = inputs[k] if part is None or part == "raw" else inputs[k].at[part]
-            copies.append(
-                None if part == "raw" else pltpu.make_async_copy(source, held[k], arrival.at[k])
-            )
-
-        def begin(k):
-            if k not in begun:
-                copies[k].start()
-                begun.add(k)
-
-        def load(k):
-            if copies[k] is None:
-                return inputs[k]
-            begin(k)
-            if k not in waited:
-                copies[k].wait()
-                waited.add(k)
-            return held[k]
-
-        load.begin = begin
-        for k in range(many):
-            if k not in late and copies[k] is not None:
+
+        def act(work, idle=False):
+            copies, begun, waited, started = [], set(), set(), []
+            for k, (one, part) in enumerate(operands):
+                if part == "raw":
+                    copies.append(None)
+                    continue
+                source = inputs[k] if part is None else inputs[k].at[part]
+                copies.append(pltpu.make_async_copy(source, held[k], arrival.at[k]))
+
+            def begin(k):
+                if k not in begun:
+                    copies[k].start()
+                    begun.add(k)
+
+            def load(k):
+                if copies[k] is None:
+                    return inputs[k]
                 begin(k)
-
-        def store(k, part=None):
-            source, target = made[k], results[k]
-            if part is not None:
-                source, target = source.at[part], target.at[part]
-            started.append(pltpu.make_async_copy(source, target, departure.at[len(started)]))
-            started[-1].start()
-
-        body(given, load, made, store, *refs)
-        for k in range(many):
-            load(k)
-        for copy in started:
-            copy.wait()
+                if k not in waited:
+                    copies[k].wait()
+                    waited.add(k)
+                return held[k]
+
+            def store(k, part=None):
+                source, target = made[k], results[k]
+                if part is not None:
+                    source, target = source.at[part], target.at[part]
+                started.append(pltpu.make_async_copy(source, target, departure.at[len(started)]))
+                started[-1].start()
+
+            load.begin = begin
+            if not idle:
+                for k in range(many):
+                    if k not in late and copies[k] is not None:
+                        begin(k)
+            work(given, load, made, store, *refs)
+            if not idle:
+                for k in range(many):
+                    load(k)
+            for copy in started:
+                copy.wait()
+
+        if when is None:
+            act(body)
+            return
+        pl.when(when(given))(lambda: act(body))
+        if other is not None:
+            pl.when(jnp.logical_not(when(given)))(lambda: act(other, True))
 
     made_here = pl.pallas_call(
         run,
@@ -316,10 +326,7 @@
         v_ref[power + 1, 0], v_ref[power + 1, 1] = split(times_upper(value, base))
         return carry
 
-    @pl.when((at[7] >= 0) & (at[7] < FRONTS))
-    def _():
-        lax.fori_loop(0, 2, squared, 0)
-
+    lax.fori_loop(0, 2, squared, 0)
     for power in (1, 2):
         store(0, power)
         store(1, power)
@@ -340,45 +347,28 @@
     solved_ref, sent_ref, mine_ref, give_ref = made[:4]
     width = solved_ref.shape[0]
     half = width // 2
-    core, root = at[1], at[6]
+    core = at[1]
     base = 3 + 5 * count
-    for k in range(base):
+    for k in range(2, base):
         load(k)
     load.begin(base)
     load.begin(base + 1)
+    source = load(2)[...]
+    for n in range(count):
+        a_at, down_at, right_at, keep_at, got_at = range(3 + 5 * n, 8 + 5 * n)
+        source = source - narrow(square_of(load(a_at)), load(down_at)[...])
+        b_tile = joined(b_scr.at[n], core, load(keep_at), load(got_at))
+        source = source - narrow(load(right_at)[...], b_tile)
     u_ref, v_ref = load(0), load(1)
-
-    @pl.when(root > 0)
-    def _():
-        source = load(2)[...]
-        for n in range(count):
-            a_at, down_at, right_at, keep_at, got_at = range(3 + 5 * n, 8 + 5 * n)
-            source = source - narrow(square_of(load(a_at)), load(down_at)[...])
-            b_tile = joined(b_scr.at[n], core, load(keep_at), load(got_at))
-            source = source - narrow(load(right_at)[...], b_tile)
-        begun(source, (u_ref[0], u_ref[1]), (v_ref[0], v_ref[1]), scale[0], solved_ref)
-
-    u_high, v_high = load(base), load(base + 1)
-
-    @pl.when(root > 0)
-    def _():
-        doubled(u_high, v_high, solved_ref)
-        sent_ref[...] = solved_ref[...].astype(half_type)
-
+    begun(source, (u_ref[0], u_ref[1]), (v_ref[0], v_ref[1]), scale[0], solved_ref)
+    doubled(load(base), load(base + 1), solved_ref)
+    sent_ref[...] = solved_ref[...].astype(half_type)
     store(1)
+    store(0)
     tiles = [sent_ref] if mine_ref.shape[0] == 1 else [load(4), sent_ref]
     for n, tile in enumerate(tiles):
-
-        @pl.when(root > 0)
-        def _():
-            mine_ref[n] = tile[pl.ds(core * half, half)]
-            give_ref[n] = tile[pl.ds((1 - core) * half, half)]
-
-        @pl.when(root == 0)
-        def _():
-            mine_ref[n] = jnp.zeros((half, width), half_type)
-            give_ref[n] = jnp.zeros((half, width), half_type)
-
+        mine_ref[n] = tile[pl.ds(core * half, half)]
+        give_ref[n] = tile[pl.ds((1 - core) * half, half)]
     if len(made) > 4:
         cols, twice, _ = made[4].shape
         strip = twice // 2
@@ -387,7 +377,12 @@
         store(4)
     store(3)
     store(2)
-    store(0)
+
+
+def nothing_sent(scalars, load, made, store, b_scr):
+    for k in (2, 3):
+        made[k][...] = jnp.zeros(made[k].shape, half_type)
+        store(k)
 
 
 def packed_body(scalars, load, made, store, piece, arrival):
@@ -398,9 +393,10 @@
     come = pltpu.make_async_copy(load(0).at[at[2]], piece, arrival.at[0])
     come.start()
     out_ref[:, 2 * strip :] = load(1)[...].reshape(cols, strip, -1)
+    store(0, (slice(None), slice(2 * strip, 3 * strip)))
     come.wait()
     out_ref[:, : 2 * strip] = jnp.broadcast_to(piece[...], (cols, *piece.shape))
-    store(0)
+    store(0, (slice(None), slice(0, 2 * strip)))
 
 
 def fanned_body(scalars, load, made, store, piece, arrival):
@@ -525,6 +521,7 @@
         [powers, powers, (tile, full_type), (tile, half_type)],
         v_here, v_there, (opened, (slice(None), slice(0, 2 * strip))), work,
         scalars=(at, scale), scratch=[pltpu.VMEM((2, rows, strip, width), half_type)],
+        when=lambda given: (given[0][7] >= 0) & (given[0][7] < FRONTS),
     )
     hop_down = send(s_first, grid.moved(first, 1, 0))
     hop_right = send(s_first, grid.moved(first, 0, 1))
@@ -551,6 +548,7 @@
         [(tile, full_type), (tile, half_type), both, both, ((cols, 2 * strip, width), half_type)],
         (u_list, 0), (v_list, 0), work, a_of(0), hop_down, hop_right, (b_keep, 0), (b_got, 0), *more,
         scalars=(at_second, scale), scratch=[b_more], late=(8, 9),
+        when=lambda given: given[0][6] > 0, other=nothing_sent,
     )
     hop_down = send(s_second, grid.moved(first + 1, 1, 0))
     hop_right = send(s_second, grid.moved(first + 1, 0, 1))
@@ -563,6 +561,7 @@
         a_of(0), far_down, far_right, (b_keep, 0), (b_got, 0),
         a_of(1), hop_down, hop_right, (b_keep, 1), (b_got, 1), *more,
         scalars=(at_last, scale), scratch=[b_more], late=(13, 14),
+        when=lambda given: given[0][6] > 0, other=nothing_sent,
     )
     one = pltpu.SemaphoreType.DMA((1,))
     (fourth_operand,) = kernel(

time: 216 us -> 216 us (level)
  starting transfers between devices: 122 us -> 137 us
  Pallas kernels: 45.5 us -> 30.7 us
    all_to_all x4, starting transfers between devices: 71.2 us -> 86.1 us  [exchange(): return lax.all_to_all(array, axis, split_axis=0, concat_axis=0, tiled=True)]
    pallas_call x10, Pallas kernels: 45.5 us -> 30.7 us  [kernel(): pl.pallas_call(run, out_shape=[PLACE(shape, kind) for shape, kind in outs...]
  transfers between devices with their start and end apart: 36 -> 36, of which waited for: 5 -> 5; matrix products, arithmetic and copies ran while one was open for 4% -> 4% of each run, Pallas kernels for 14% -> 10%
where the time goes in v3:
time: 216 us; the launch traced here: 214 us
  starting transfers between devices  137 us (63%)
  waiting for transfers between devices  32.4 us (15%)
  Pallas kernels  30.7 us (14%)
  other arithmetic  7.36 us (3%)
  local copies, waits for them, and re-layouts  4.71 us (2%)
    all_to_all x4, starting transfers between devices, exchange(): return lax.all_to_all(array, axis, split_axis=0, concat_axis=0, tiled=True)  86.1 us
    ppermute x32, starting transfers between devices, send(): return lax.ppermute(array, ('row', 'col'), pairs)  51.3 us
    ppermute x32, waiting for transfers between devices, send(): return lax.ppermute(array, ('row', 'col'), pairs)  32.4 us
    pallas_call x10, Pallas kernels, kernel(): pl.pallas_call(run, out_shape=[PLACE(shape, kind) for shape, kind in outs...  30.7 us
    unnamed x26, local copies, waits for them, and re-layouts  4.46 us
    add x6, other arithmetic, spread_deep(): held = held + got  4.38 us
  transfers between devices with their start and end apart: 36, of which 5 were waited for; matrix products, arithmetic and copies ran while one was open for 4% of the time, Pallas kernels for 10%

profile of v3, /device:TPU:70, one launch (start us, length us, event | category | flops | bytes accessed | tf_op | source)
XLA Modules:
  0.0 214.0 jit_solution(12581636451353756093)
XLA Ops:
  0.1 3.9 %shard_map.64 = (bf16[16,160,512]{2,1,0:T(8,128)(2,1)}, bf16[64,512]{1,0:T(8,128)(2,1)}, bf16[128,512]{1,0:T(8,128)(2,1)}, bf16[128,512]{1,0:T(8,128)(2,1)}, bf1...) custom-call(s32[8]{0:T(128)S(1)} %stack.87.refs_0_, ...), custom_call_target="tpu_custom_call" | custom-call | tf_op jit(solution)/shard_map/pallas_call | solution.py:171
  4.1 7.6 %all-to-all-start = ((bf16[16,160,512]{2,1,0:T(8,128)(2,1)}), bf16[16,160,512]{2,1,0:T(8,128)(2,1)S(1)}, u32[]{:S(2)}, u32[]{:S(2)}) async-start(bf16[16,160,512]{2,1,0:T(8,128)(2,1)} %get-tuple-element.31), calls=%async_computation | async-start | bytes 5242880 | tf_op jit(solution)/shard_map/all_to_all | solution.py:86
  11.6 2.0 collective-permute-start.6
  13.7 1.3 collective-permute-start.5
  18.4 4.7 %collective-permute-start.10 = (bf16[128,512]{1,0:T(8,128)(2,1)}, bf16[128,512]{1,0:T(8,128)(2,1)S(1)}, u32[]{:S(2)}, u32[]{:S(2)}) collective-permute-start(bf16[128,512]{1,0:T(8,128)(2,1)} %get-tuple-element.37), channel_id=1, source_target_pairs={{11,43},{12,44},{13,45},{14,46},{15,47},{27,59},{28,60},{29,61},{3... | collective-permute-start | bytes 393224 | tf_op jit(solution)/shard_map/ppermute | solution.py:90
  23.1 6.7 %collective-permute-start.11 = (bf16[128,512]{1,0:T(8,128)(2,1)S(1)}, bf16[128,512]{1,0:T(8,128)(2,1)S(1)}, u32[]{:S(2)}, u32[]{:S(2)}) collective-permute-start(bf16[128,512]{1,0:T(8,128)(2,1)S(1)} %copy-done.12), channel_id=1, source_target_pairs={{9,73},{10,74},{11,75},{12,76},{13,77},{14,78},{15,79},{25,89},{26... | collective-permute-start | bytes 393224 | tf_op jit(solution)/shard_map/ppermute | solution.py:90
  29.9 2.5 %collective-permute-start.12 = (bf16[128,512]{1,0:T(8,128)(2,1)S(1)}, bf16[128,512]{1,0:T(8,128)(2,1)S(1)}, u32[]{:S(2)}, u32[]{:S(2)}) collective-permute-start(bf16[128,512]{1,0:T(8,128)(2,1)S(1)} %copy-done.11), channel_id=1, source_target_pairs={{7,103},{8,104},{9,105},{10,106},{11,107},{12,108},{13,109},{14,11... | collective-permute-start | bytes 393224 | tf_op jit(solution)/shard_map/ppermute | solution.py:90
  32.4 2.6 %shard_map.65.refs_2_ = bf16[8,64,512]{2,1,0:T(8,128)(2,1)} custom-call(s32[8]{0:T(128)S(1)} %stack.87.refs_0_, bf16[64,512]{1,0:T(8,128)(2,1)} %get-tuple-element.30.refs_1_, bf16[64,512]{1,0:T(8,128)(2,1)S(1)} %collective-permute-done.refs_2_, bf16[64,512]{1,0:T(8,128)(2,1)S(1)} %collective-permute-done.1.refs_3_, ...), custom_call_target="tpu_custom_call" | custom-call | tf_op jit(solution)/shard_map/pallas_call | solution.py:171
  35.1 5.7 %collective-permute-start.13 = (bf16[128,512]{1,0:T(8,128)(2,1)S(1)}, bf16[128,512]{1,0:T(8,128)(2,1)S(1)}, u32[]{:S(2)}, u32[]{:S(2)}) collective-permute-start(bf16[128,512]{1,0:T(8,128)(2,1)S(1)} %copy-done.10), channel_id=1, source_target_pairs={{5,133},{6,134},{7,135},{8,136},{9,137},{10,138},{11,139},{12,140}... | collective-permute-start | bytes 393224 | tf_op jit(solution)/shard_map/ppermute | solution.py:90
  40.8 3.2 %collective-permute-start.14 = (bf16[128,512]{1,0:T(8,128)(2,1)S(1)}, bf16[128,512]{1,0:T(8,128)(2,1)S(1)}, u32[]{:S(2)}, u32[]{:S(2)}) collective-permute-start(bf16[128,512]{1,0:T(8,128)(2,1)S(1)} %copy-done.9), channel_id=1, source_target_pairs={{3,163},{4,164},{5,165},{6,166},{7,167},{8,168},{9,169},{10,170},{... | collective-permute-start | bytes 393224 | tf_op jit(solution)/shard_map/ppermute | solution.py:90
  44.0 3.3 %collective-permute-done.11.refs_3_ = bf16[128,512]{1,0:T(8,128)(2,1)S(1)} collective-permute-done((bf16[128,512]{1,0:T(8,128)(2,1)S(1)}, bf16[128,512]{1,0:T(8,128)(2,1)S(1)}, u32[]{:S(2)}, u32[]{:S(2)}) %collective-permute-start.11) | collective-permute-done | bytes 131104 | tf_op jit(solution)/shard_map/ppermute | solution.py:90
  47.4 1.3 collective-permute-start.15
  48.7 1.9 collective-permute-start.16
  50.6 7.6 %collective-permute-done.14.refs_6_ = bf16[128,512]{1,0:T(8,128)(2,1)S(1)} collective-permute-done((bf16[128,512]{1,0:T(8,128)(2,1)S(1)}, bf16[128,512]{1,0:T(8,128)(2,1)S(1)}, u32[]{:S(2)}, u32[]{:S(2)}) %collective-permute-start.14) | collective-permute-done | bytes 131104 | tf_op jit(solution)/shard_map/ppermute | solution.py:90
  58.2 5.7 %collective-permute-done.15.refs_7_ = bf16[128,512]{1,0:T(8,128)(2,1)S(1)} collective-permute-done((bf16[128,512]{1,0:T(8,128)(2,1)S(1)}, bf16[128,512]{1,0:T(8,128)(2,1)S(1)}, u32[]{:S(2)}, u32[]{:S(2)}) %collective-permute-start.15) | collective-permute-done | bytes 131104 | tf_op jit(solution)/shard_map/ppermute | solution.py:90
  63.9 3.3 %shard_map.67 = (bf16[3,8,32,512]{3,2,1,0:T(8,128)(2,1)}, bf16[3,8,32,512]{3,2,1,0:T(8,128)(2,1)}) custom-call(s32[8]{0:T(128)S(1)} %stack.87.refs_0_, bf16[128,512]{1,0:T(8,128)(2,1)} %get-tuple-element.36.refs_1_, bf16[128,512]{1,0:T(8,128)(2,1)S(1)} %collective-permute-done.10.refs_2_, bf16[128,512]{1,0:T(8,128)(2,1)S(1)} %collective-permute-done.11.refs_3_, ...), custom_call_target="tpu_custom_call" | custom-call | tf_op jit(solution)/shard_map/pallas_call | solution.py:171
  68.8 1.0 copy-done.3
  69.9 0.8 shard_map.66
  70.7 1.5 collective-permute-start.9
  72.2 1.5 collective-permute-start.8
  73.7 2.1 shard_map.68
  75.8 36.1 %all-to-all-start.1 = ((bf16[16,64,512]{2,1,0:T(8,128)(2,1)}), bf16[16,64,512]{2,1,0:T(8,128)(2,1)}, u32[]{:S(2)}, u32[]{:S(2)}) async-start(bf16[16,64,512]{2,1,0:T(8,128)(2,1)} %get-tuple-element.51), calls=%async_computation.1 | async-start | bytes 2097152 | tf_op jit(solution)/shard_map/all_to_all | solution.py:86
  111.9 1.5 collective-permute-start.19
  113.4 1.5 collective-permute-start.18
  114.9 1.5 collective-permute-start.21
  116.3 1.4 collective-permute-start.20
  117.8 2.0 add.35
  119.7 1.5 collective-permute-start.23
  121.3 1.7 shard_map.69
  123.1 3.0 %shard_map.70 = bf16[16,96,512]{2,1,0:T(8,128)(2,1)} custom-call(s32[8]{0:T(128)S(1)} %stack.91.refs_0_, bf16[16,64,512]{2,1,0:T(8,128)(2,1)} %all-to-all-done.1.refs_1_, bf16[512,512]{1,0:T(8,128)(2,1)} %get-tuple-element.52.refs_2_), custom_call_target="tpu_custom_call" | custom-call | tf_op jit(solution)/shard_map/pallas_call | solution.py:171
  126.1 26.5 %all-to-all-start.2 = ((bf16[16,96,512]{2,1,0:T(8,128)(2,1)}), bf16[16,96,512]{2,1,0:T(8,128)(2,1)}, u32[]{:S(2)}, u32[]{:S(2)}) async-start(bf16[16,96,512]{2,1,0:T(8,128)(2,1)} %shard_map.70), calls=%async_computation.2 | async-start | bytes 3145728 | tf_op jit(solution)/shard_map/all_to_all | solution.py:86
  152.6 1.3 add.36
  154.7 1.5 collective-permute-start.27
  156.2 1.4 collective-permute-done.27
  157.5 1.0 add.39
  158.7 1.3 collective-permute-start.25
  161.5 14.3 %collective-permute-done.25 = bf16[2,256,512]{2,1,0:T(8,128)(2,1)S(1)} collective-permute-done((bf16[2,256,512]{2,1,0:T(8,128)(2,1)S(1)}, bf16[2,256,512]{2,1,0:T(8,128)(2,1)S(1)}, u32[]{:S(2)}, u32[]{:S(2)}) %collective-permute-start.25) | collective-permute-done | bytes 524320 | tf_op jit(solution)/shard_map/ppermute | solution.py:90
  175.8 0.9 add.38.refs_6_.refs_12_
  176.7 0.8 add.41
  177.5 1.3 collective-permute-start.30
  178.8 2.4 %shard_map.72 = bf16[16,32,512]{2,1,0:T(8,128)(2,1)} custom-call(s32[8]{0:T(128)S(1)} %stack.95.refs_0_, bf16[16,96,512]{2,1,0:T(8,128)(2,1)} %all-to-all-done.2.refs_8_.refs_14_.refs_1_), custom_call_target="tpu_custom_call" | custom-call | tf_op jit(solution)/shard_map/pallas_call | solution.py:171
  181.2 15.9 %all-to-all-start.3 = ((bf16[16,32,512]{2,1,0:T(8,128)(2,1)}), bf16[16,32,512]{2,1,0:T(8,128)(2,1)}, u32[]{:S(2)}, u32[]{:S(2)}) async-start(bf16[16,32,512]{2,1,0:T(8,128)(2,1)} %shard_map.72), calls=%async_computation.3 | async-start | bytes 1048576 | tf_op jit(solution)/shard_map/all_to_all | solution.py:86
  197.1 1.1 add.42.refs_3_
  198.2 2.1 collective-permute-start.31
  200.3 6.7 %shard_map.71.refs_1_ = f32[512,512]{1,0:T(8,128)} custom-call(s32[8]{0:T(128)S(1)} %stack.87.refs_0_, f32[512,512]{1,0:T(8,128)} %refs_1_.3, f32[512,512]{1,0:T(8,128)} %get-tuple-element.32.refs_2_, f32[512,512]{1,0:T(8,128)} %get-tuple-element.46.refs_3_, f32[512,512]{1,0:T(8,128)} %get-tuple-element.48.refs_4_, ...), custom_call_target="tpu_custom_call" | custom-call | tf_op jit(solution)/shard_map/pallas_call | solution.py:171
  207.7 0.9 copy-done.1
  208.7 0.9 copy-done.5
  209.6 4.2 %shard_map.73 = f32[512,512]{1,0:T(8,128)} custom-call(s32[8]{0:T(128)S(1)} %stack.87.refs_0_, f32[512,512]{1,0:T(8,128)} %shard_map.71.refs_1_, bf16[16,160,512]{2,1,0:T(8,128)(2,1)S(1)} %all-to-all-done.refs_4_.refs_5_.refs_10_.refs_11_.refs_2_, bf16[1,256,512]{2,1,0:T(8,128)(2,1)S(1)} %copy-done.1, bf16[1,256,512]{2,1,0:T(8,128)(2,1)S(1)} %copy-done.5, ...), custom_call_target="tpu_custom_call" | custom-call | tf_op jit(solution)/shard_map/pallas_call | solution.py:171
  (71 shorter events, 7.6 us)
Async XLA Ops:
  4.0 7.6 %copy-start.6 = (bf16[64,512]{1,0:T(8,128)(2,1)S(1)}, bf16[64,512]{1,0:T(8,128)(2,1)}, u32[]{:S(2)}) copy-start(bf16[64,512]{1,0:T(8,128)(2,1)} %get-tuple-element.30.refs_1_) | copy-start | bytes 196612
  4.0 19.1 %copy-start.12 = (bf16[128,512]{1,0:T(8,128)(2,1)S(1)}, bf16[128,512]{1,0:T(8,128)(2,1)}, u32[]{:S(2)}) copy-start(bf16[128,512]{1,0:T(8,128)(2,1)} %get-tuple-element.38) | copy-start | bytes 393220
  4.0 25.9 %copy-start.11 = (bf16[128,512]{1,0:T(8,128)(2,1)S(1)}, bf16[128,512]{1,0:T(8,128)(2,1)}, u32[]{:S(2)}) copy-start(bf16[128,512]{1,0:T(8,128)(2,1)} %get-tuple-element.39) | copy-start | bytes 393220
  4.0 31.1 %copy-start.10 = (bf16[128,512]{1,0:T(8,128)(2,1)S(1)}, bf16[128,512]{1,0:T(8,128)(2,1)}, u32[]{:S(2)}) copy-start(bf16[128,512]{1,0:T(8,128)(2,1)} %get-tuple-element.40) | copy-start | bytes 393220
  4.0 36.8 %copy-start.9 = (bf16[128,512]{1,0:T(8,128)(2,1)S(1)}, bf16[128,512]{1,0:T(8,128)(2,1)}, u32[]{:S(2)}) copy-start(bf16[128,512]{1,0:T(8,128)(2,1)} %get-tuple-element.41) | copy-start | bytes 393220
  4.0 43.3 %copy-start.8 = (bf16[128,512]{1,0:T(8,128)(2,1)S(1)}, bf16[128,512]{1,0:T(8,128)(2,1)}, u32[]{:S(2)}) copy-start(bf16[128,512]{1,0:T(8,128)(2,1)} %get-tuple-element.42) | copy-start | bytes 393220
  4.0 44.6 %copy-start.7 = (bf16[128,512]{1,0:T(8,128)(2,1)S(1)}, bf16[128,512]{1,0:T(8,128)(2,1)}, u32[]{:S(2)}) copy-start(bf16[128,512]{1,0:T(8,128)(2,1)} %get-tuple-element.43) | copy-start | bytes 393220
  4.1 64.8 %all-to-all-start = ((bf16[16,160,512]{2,1,0:T(8,128)(2,1)}), bf16[16,160,512]{2,1,0:T(8,128)(2,1)S(1)}, u32[]{:S(2)}, u32[]{:S(2)}) async-start(bf16[16,160,512]{2,1,0:T(8,128)(2,1)} %get-tuple-element.31), calls=%async_computation | async-start | bytes 5242880 | tf_op jit(solution)/shard_map/all_to_all | solution.py:86
  11.6 5.3 %collective-permute-start.6 = (bf16[64,512]{1,0:T(8,128)(2,1)S(1)}, bf16[64,512]{1,0:T(8,128)(2,1)S(1)}, u32[]{:S(2)}, u32[]{:S(2)}) collective-permute-start(bf16[64,512]{1,0:T(8,128)(2,1)S(1)} %copy-done.6), channel_id=1, source_target_pairs={{0,224},{1,225},{16,240},{17,241},{44,12},{45,13},{46,14},{47,15},... | collective-permute-start | bytes 196616 | tf_op jit(solution)/shard_map/ppermute | solution.py:90
  13.7 4.0 %collective-permute-start.5 = (bf16[64,512]{1,0:T(8,128)(2,1)S(1)}, bf16[64,512]{1,0:T(8,128)(2,1)S(1)}, u32[]{:S(2)}, u32[]{:S(2)}) collective-permute-start(bf16[64,512]{1,0:T(8,128)(2,1)S(1)} %copy-done.6), channel_id=1, source_target_pairs={{0,192},{1,193},{2,194},{3,195},{16,208},{17,209},{18,210},{19,211... | collective-permute-start | bytes 196616 | tf_op jit(solution)/shard_map/ppermute | solution.py:90
  15.0 3.4 %collective-permute-start.4 = (bf16[64,512]{1,0:T(8,128)(2,1)S(1)}, bf16[64,512]{1,0:T(8,128)(2,1)S(1)}, u32[]{:S(2)}, u32[]{:S(2)}) collective-permute-start(bf16[64,512]{1,0:T(8,128)(2,1)S(1)} %copy-done.6), channel_id=1, source_target_pairs={{2,162},{3,163},{4,164},{5,165},{18,178},{19,179},{20,180},{21,181... | collective-permute-start | bytes 196616 | tf_op jit(solution)/shard_map/ppermute | solution.py:90
  15.6 7.5 %collective-permute-start.3 = (bf16[64,512]{1,0:T(8,128)(2,1)S(1)}, bf16[64,512]{1,0:T(8,128)(2,1)S(1)}, u32[]{:S(2)}, u32[]{:S(2)}) collective-permute-start(bf16[64,512]{1,0:T(8,128)(2,1)S(1)} %copy-done.6), channel_id=1, source_target_pairs={{4,132},{5,133},{6,134},{7,135},{20,148},{21,149},{22,150},{23,151... | collective-permute-start | bytes 196616 | tf_op jit(solution)/shard_map/ppermute | solution.py:90
  16.3 13.5 %collective-permute-start.2 = (bf16[64,512]{1,0:T(8,128)(2,1)S(1)}, bf16[64,512]{1,0:T(8,128)(2,1)S(1)}, u32[]{:S(2)}, u32[]{:S(2)}) collective-permute-start(bf16[64,512]{1,0:T(8,128)(2,1)S(1)} %copy-done.6), channel_id=1, source_target_pairs={{6,102},{7,103},{8,104},{9,105},{22,118},{23,119},{24,120},{25,121... | collective-permute-start | bytes 196616 | tf_op jit(solution)/shard_map/ppermute | solution.py:90
  17.0 15.4 %collective-permute-start.1 = (bf16[64,512]{1,0:T(8,128)(2,1)S(1)}, bf16[64,512]{1,0:T(8,128)(2,1)S(1)}, u32[]{:S(2)}, u32[]{:S(2)}) collective-permute-start(bf16[64,512]{1,0:T(8,128)(2,1)S(1)} %copy-done.6), channel_id=1, source_target_pairs={{8,72},{9,73},{10,74},{11,75},{24,88},{25,89},{26,90},{27,91},{38,... | collective-permute-start | bytes 196616 | tf_op jit(solution)/shard_map/ppermute | solution.py:90
  17.7 14.8 %collective-permute-start = (bf16[64,512]{1,0:T(8,128)(2,1)S(1)}, bf16[64,512]{1,0:T(8,128)(2,1)S(1)}, u32[]{:S(2)}, u32[]{:S(2)}) collective-permute-start(bf16[64,512]{1,0:T(8,128)(2,1)S(1)} %copy-done.6), channel_id=1, source_target_pairs={{10,42},{11,43},{12,44},{13,45},{26,58},{27,59},{28,60},{29,61},{4... | collective-permute-start | bytes 196616 | tf_op jit(solution)/shard_map/ppermute | solution.py:90
  18.4 22.5 %collective-permute-start.10 = (bf16[128,512]{1,0:T(8,128)(2,1)}, bf16[128,512]{1,0:T(8,128)(2,1)S(1)}, u32[]{:S(2)}, u32[]{:S(2)}) collective-permute-start(bf16[128,512]{1,0:T(8,128)(2,1)} %get-tuple-element.37), channel_id=1, source_target_pairs={{11,43},{12,44},{13,45},{14,46},{15,47},{27,59},{28,60},{29,61},{3... | collective-permute-start | bytes 393224 | tf_op jit(solution)/shard_map/ppermute | solution.py:90
  23.1 24.2 %collective-permute-start.11 = (bf16[128,512]{1,0:T(8,128)(2,1)S(1)}, bf16[128,512]{1,0:T(8,128)(2,1)S(1)}, u32[]{:S(2)}, u32[]{:S(2)}) collective-permute-start(bf16[128,512]{1,0:T(8,128)(2,1)S(1)} %copy-done.12), channel_id=1, source_target_pairs={{9,73},{10,74},{11,75},{12,76},{13,77},{14,78},{15,79},{25,89},{26... | collective-permute-start | bytes 393224 | tf_op jit(solution)/shard_map/ppermute | solution.py:90
  29.9 18.8 %collective-permute-start.12 = (bf16[128,512]{1,0:T(8,128)(2,1)S(1)}, bf16[128,512]{1,0:T(8,128)(2,1)S(1)}, u32[]{:S(2)}, u32[]{:S(2)}) collective-permute-start(bf16[128,512]{1,0:T(8,128)(2,1)S(1)} %copy-done.11), channel_id=1, source_target_pairs={{7,103},{8,104},{9,105},{10,106},{11,107},{12,108},{13,109},{14,11... | collective-permute-start | bytes 393224 | tf_op jit(solution)/shard_map/ppermute | solution.py:90
  35.0 33.0 %collective-permute-start.7 = (bf16[8,64,512]{2,1,0:T(8,128)(2,1)}, bf16[8,64,512]{2,1,0:T(8,128)(2,1)S(1)}, u32[]{:S(2)}, u32[]{:S(2)}) collective-permute-start(bf16[8,64,512]{2,1,0:T(8,128)(2,1)} %shard_map.65.refs_2_), channel_id=1, source_target_pairs={{0,16},{1,17},{2,18},{3,19},{4,20},{5,21},{6,22},{7,23},{8,24},{9,... | collective-permute-start | bytes 1572872 | tf_op jit(solution)/shard_map/ppermute | solution.py:90
  35.1 15.5 %collective-permute-start.13 = (bf16[128,512]{1,0:T(8,128)(2,1)S(1)}, bf16[128,512]{1,0:T(8,128)(2,1)S(1)}, u32[]{:S(2)}, u32[]{:S(2)}) collective-permute-start(bf16[128,512]{1,0:T(8,128)(2,1)S(1)} %copy-done.10), channel_id=1, source_target_pairs={{5,133},{6,134},{7,135},{8,136},{9,137},{10,138},{11,139},{12,140}... | collective-permute-start | bytes 393224 | tf_op jit(solution)/shard_map/ppermute | solution.py:90
  40.8 17.4 %collective-permute-start.14 = (bf16[128,512]{1,0:T(8,128)(2,1)S(1)}, bf16[128,512]{1,0:T(8,128)(2,1)S(1)}, u32[]{:S(2)}, u32[]{:S(2)}) collective-permute-start(bf16[128,512]{1,0:T(8,128)(2,1)S(1)} %copy-done.9), channel_id=1, source_target_pairs={{3,163},{4,164},{5,165},{6,166},{7,167},{8,168},{9,169},{10,170},{... | collective-permute-start | bytes 393224 | tf_op jit(solution)/shard_map/ppermute | solution.py:90
  47.4 16.6 %collective-permute-start.15 = (bf16[128,512]{1,0:T(8,128)(2,1)S(1)}, bf16[128,512]{1,0:T(8,128)(2,1)S(1)}, u32[]{:S(2)}, u32[]{:S(2)}) collective-permute-start(bf16[128,512]{1,0:T(8,128)(2,1)S(1)} %copy-done.8), channel_id=1, source_target_pairs={{1,193},{2,194},{3,195},{4,196},{5,197},{6,198},{7,199},{8,200},{9... | collective-permute-start | bytes 393224 | tf_op jit(solution)/shard_map/ppermute | solution.py:90
  48.7 15.3 %collective-permute-start.16 = (bf16[128,512]{1,0:T(8,128)(2,1)S(1)}, bf16[128,512]{1,0:T(8,128)(2,1)S(1)}, u32[]{:S(2)}, u32[]{:S(2)}) collective-permute-start(bf16[128,512]{1,0:T(8,128)(2,1)S(1)} %copy-done.7), channel_id=1, source_target_pairs={{0,224},{1,225},{2,226},{3,227},{4,228},{5,229},{6,230},{7,231},{8... | collective-permute-start | bytes 393224 | tf_op jit(solution)/shard_map/ppermute | solution.py:90
  67.2 6.5 %collective-permute-start.17 = (bf16[3,8,32,512]{3,2,1,0:T(8,128)(2,1)}, bf16[3,8,32,512]{3,2,1,0:T(8,128)(2,1)S(1)}, u32[]{:S(2)}, u32[]{:S(2)}) collective-permute-start(bf16[3,8,32,512]{3,2,1,0:T(8,128)(2,1)} %get-tuple-element.45), channel_id=1, source_target_pairs={{0,16},{1,17},{2,18},{3,19},{4,20},{5,21},{6,22},{7,23},{8,24},{9,... | collective-permute-start | bytes 2359304 | tf_op jit(solution)/shard_map/ppermute | solution.py:90
  68.0 0.8 copy-start.2
  68.8 1.0 copy-start.3
  70.7 3.0 %collective-permute-start.9 = (bf16[512,512]{1,0:T(8,128)(2,1)}, bf16[512,512]{1,0:T(8,128)(2,1)}, u32[]{:S(2)}, u32[]{:S(2)}) collective-permute-start(bf16[512,512]{1,0:T(8,128)(2,1)} %get-tuple-element.35), channel_id=1, source_target_pairs={{13,14},{28,29},{43,44},{58,59},{73,74},{88,89},{103,104},{118,119... | collective-permute-start | bytes 1572872 | tf_op jit(solution)/shard_map/ppermute | solution.py:90
  72.2 1.6 collective-permute-start.8
  75.8 47.2 %all-to-all-start.1 = ((bf16[16,64,512]{2,1,0:T(8,128)(2,1)}), bf16[16,64,512]{2,1,0:T(8,128)(2,1)}, u32[]{:S(2)}, u32[]{:S(2)}) async-start(bf16[16,64,512]{2,1,0:T(8,128)(2,1)} %get-tuple-element.51), calls=%async_computation.1 | async-start | bytes 2097152 | tf_op jit(solution)/shard_map/all_to_all | solution.py:86
  111.9 5.9 %collective-permute-start.22 = (bf16[2,256,512]{2,1,0:T(8,128)(2,1)}, bf16[2,256,512]{2,1,0:T(8,128)(2,1)S(1)}, u32[]{:S(2)}, u32[]{:S(2)}) collective-permute-start(bf16[2,256,512]{2,1,0:T(8,128)(2,1)} %get-tuple-element.50), channel_id=1, source_target_pairs={{0,16},{1,17},{2,18},{3,19},{4,20},{5,21},{6,22},{7,23},{8,24},{9,... | collective-permute-start | bytes 1572872 | tf_op jit(solution)/shard_map/ppermute | solution.py:90
  111.9 9.4 %collective-permute-start.19 = (bf16[512,512]{1,0:T(8,128)(2,1)}, bf16[512,512]{1,0:T(8,128)(2,1)}, u32[]{:S(2)}, u32[]{:S(2)}) collective-permute-start(bf16[512,512]{1,0:T(8,128)(2,1)} %get-tuple-element.35), channel_id=1, source_target_pairs={{13,15},{28,30},{43,45},{58,60},{73,75},{88,90},{103,105},{118,120... | collective-permute-start | bytes 1572872 | tf_op jit(solution)/shard_map/ppermute | solution.py:90
  113.4 7.9 %collective-permute-start.18 = (bf16[512,512]{1,0:T(8,128)(2,1)}, bf16[512,512]{1,0:T(8,128)(2,1)}, u32[]{:S(2)}, u32[]{:S(2)}) collective-permute-start(bf16[512,512]{1,0:T(8,128)(2,1)} %get-tuple-element.35), channel_id=1, source_target_pairs={{13,45},{28,60},{43,75},{58,90},{73,105},{88,120},{103,135},{118,1... | collective-permute-start | bytes 1572872 | tf_op jit(solution)/shard_map/ppermute | solution.py:90
  114.9 6.5 %collective-permute-start.21 = (bf16[512,512]{1,0:T(8,128)(2,1)}, bf16[512,512]{1,0:T(8,128)(2,1)}, u32[]{:S(2)}, u32[]{:S(2)}) collective-permute-start(bf16[512,512]{1,0:T(8,128)(2,1)} %get-tuple-element.47), channel_id=1, source_target_pairs={{14,15},{29,30},{44,45},{59,60},{74,75},{89,90},{104,105},{119,120... | collective-permute-start | bytes 1572872 | tf_op jit(solution)/shard_map/ppermute | solution.py:90
  116.3 5.0 %collective-permute-start.20 = (bf16[512,512]{1,0:T(8,128)(2,1)}, bf16[512,512]{1,0:T(8,128)(2,1)}, u32[]{:S(2)}, u32[]{:S(2)}) collective-permute-start(bf16[512,512]{1,0:T(8,128)(2,1)} %get-tuple-element.47), channel_id=1, source_target_pairs={{14,30},{29,45},{44,60},{59,75},{74,90},{89,105},{104,120},{119,13... | collective-permute-start | bytes 1572872 | tf_op jit(solution)/shard_map/ppermute | solution.py:90
  119.7 32.9 %collective-permute-start.23 = (bf16[2,256,512]{2,1,0:T(8,128)(2,1)}, bf16[2,256,512]{2,1,0:T(8,128)(2,1)}, u32[]{:S(2)}, u32[]{:S(2)}) collective-permute-start(bf16[2,256,512]{2,1,0:T(8,128)(2,1)} %add.35), channel_id=1, source_target_pairs={{14,142},{30,158},{13,141},{29,157},{44,172},{60,188},{43,171},{59... | collective-permute-start | bytes 1572872 | tf_op jit(solution)/shard_map/ppermute | solution.py:90
  126.1 52.7 %all-to-all-start.2 = ((bf16[16,96,512]{2,1,0:T(8,128)(2,1)}), bf16[16,96,512]{2,1,0:T(8,128)(2,1)}, u32[]{:S(2)}, u32[]{:S(2)}) async-start(bf16[16,96,512]{2,1,0:T(8,128)(2,1)} %shard_map.70), calls=%async_computation.2 | async-start | bytes 3145728 | tf_op jit(solution)/shard_map/all_to_all | solution.py:86
  154.0 4.6 %collective-permute-start.24 = (bf16[2,256,512]{2,1,0:T(8,128)(2,1)S(1)}, bf16[2,256,512]{2,1,0:T(8,128)(2,1)S(1)}, u32[]{:S(2)}, u32[]{:S(2)}) collective-permute-start(bf16[2,256,512]{2,1,0:T(8,128)(2,1)S(1)} %add.36), channel_id=1, source_target_pairs={{142,206},{14,78},{158,94},{30,222},{141,205},{13,77},{157,93},{29... | collective-permute-start | bytes 1572872 | tf_op jit(solution)/shard_map/ppermute | solution.py:90
  154.7 2.9 %collective-permute-start.27 = (bf16[1,256,512]{2,1,0:T(8,128)(2,1)}, bf16[1,256,512]{2,1,0:T(8,128)(2,1)S(1)}, u32[]{:S(2)}, u32[]{:S(2)}) collective-permute-start(bf16[1,256,512]{2,1,0:T(8,128)(2,1)} %get-tuple-element.54), channel_id=1, source_target_pairs={{0,16},{1,17},{2,18},{3,19},{4,20},{5,21},{6,22},{7,23},{8,24},{9,... | collective-permute-start | bytes 786440 | tf_op jit(solution)/shard_map/ppermute | solution.py:90
  158.7 17.0 %collective-permute-start.25 = (bf16[2,256,512]{2,1,0:T(8,128)(2,1)S(1)}, bf16[2,256,512]{2,1,0:T(8,128)(2,1)S(1)}, u32[]{:S(2)}, u32[]{:S(2)}) collective-permute-start(bf16[2,256,512]{2,1,0:T(8,128)(2,1)S(1)} %add.37), channel_id=1, source_target_pairs={{206,238},{142,174},{78,110},{14,46},{94,62},{158,126},{222,190},{... | collective-permute-start | bytes 1572872 | tf_op jit(solution)/shard_map/ppermute | solution.py:90
  160.0 0.7 collective-permute-start.28
  160.8 15.9 %collective-permute-start.29 = (bf16[1,256,512]{2,1,0:T(8,128)(2,1)S(1)}, bf16[1,256,512]{2,1,0:T(8,128)(2,1)S(1)}, u32[]{:S(2)}, u32[]{:S(2)}) collective-permute-start(bf16[1,256,512]{2,1,0:T(8,128)(2,1)S(1)} %add.40), channel_id=1, source_target_pairs={{143,207},{15,79},{159,95},{31,223},{142,206},{14,78},{158,94},{30... | collective-permute-start | bytes 786440 | tf_op jit(solution)/shard_map/ppermute | solution.py:90
  176.7 23.6 %collective-permute-start.26 = (bf16[2,256,512]{2,1,0:T(8,128)(2,1)}, bf16[2,256,512]{2,1,0:T(8,128)(2,1)}, u32[]{:S(2)}, u32[]{:S(2)}) collective-permute-start(bf16[2,256,512]{2,1,0:T(8,128)(2,1)} %add.38.refs_6_.refs_12_), channel_id=1, source_target_pairs={{0,16},{1,17},{2,18},{3,19},{4,20},{5,21},{6,22},{7,23},{8,24},{9,... | collective-permute-start | bytes 1572872 | tf_op jit(solution)/shard_map/ppermute | solution.py:90
  177.5 19.6 %collective-permute-start.30 = (bf16[1,256,512]{2,1,0:T(8,128)(2,1)}, bf16[1,256,512]{2,1,0:T(8,128)(2,1)}, u32[]{:S(2)}, u32[]{:S(2)}) collective-permute-start(bf16[1,256,512]{2,1,0:T(8,128)(2,1)} %add.41), channel_id=1, source_target_pairs={{207,239},{143,175},{79,111},{15,47},{95,63},{159,127},{223,191},{... | collective-permute-start | bytes 786440 | tf_op jit(solution)/shard_map/ppermute | solution.py:90
  181.2 26.5 %all-to-all-start.3 = ((bf16[16,32,512]{2,1,0:T(8,128)(2,1)}), bf16[16,32,512]{2,1,0:T(8,128)(2,1)}, u32[]{:S(2)}, u32[]{:S(2)}) async-start(bf16[16,32,512]{2,1,0:T(8,128)(2,1)} %shard_map.72), calls=%async_computation.3 | async-start | bytes 1048576 | tf_op jit(solution)/shard_map/all_to_all | solution.py:86
  198.2 8.8 %copy-start = (bf16[1,256,512]{2,1,0:T(8,128)(2,1)}, bf16[1,256,512]{2,1,0:T(8,128)(2,1)S(1)}, u32[]{:S(2)}) copy-start(bf16[1,256,512]{2,1,0:T(8,128)(2,1)S(1)} %add.42.refs_3_) | copy-start | bytes 786436
  198.2 8.8 %collective-permute-start.31 = (bf16[1,256,512]{2,1,0:T(8,128)(2,1)S(1)}, bf16[1,256,512]{2,1,0:T(8,128)(2,1)S(1)}, u32[]{:S(2)}, u32[]{:S(2)}) collective-permute-start(bf16[1,256,512]{2,1,0:T(8,128)(2,1)S(1)} %add.42.refs_3_), channel_id=1, source_target_pairs={{0,16},{1,17},{2,18},{3,19},{4,20},{5,21},{6,22},{7,23},{8,24},{9,... | collective-permute-start | bytes 786440 | tf_op jit(solution)/shard_map/ppermute | solution.py:90
  207.7 1.0 copy-start.1
  208.7 0.9 copy-start.5
  (1 other events, 0.7 us)
